TPU v7x, 128 devices: a whole 4x4x4 slice. The times are simulated.
128 devices in a mesh: shard: 32 (over y, x, core), tensor: 4 (over z).
Axes of the slice: x: 4, y: 4, z: 4, core: 2. Of those that a mesh axis runs over, the one named last changes fastest.
Arguments:
- grads: bfloat16 [16384, 2048], P('shard', 'tensor'), may hold values from -120 to 120
- assignment: int32 [4, 32], P('tensor'), may hold values from 0 to 31, as said below
- moment: float32 [32, 2048, 512], P('shard', 'tensor'), may hold values from -6 to 6
- second: float32 [32, 2048, 512], P('shard', 'tensor'), may hold values from 0.2 to 2
- left_stats: float32 [32, 2048, 512], P('shard', 'tensor'), may hold values from -0.02 to 3.1, as said below
- right_stats: float32 [32, 2048, 512], P('shard', 'tensor'), may hold values from -0.02 to 3.1, as said below
- left_basis: float32 [32, 2048, 512], P('shard', 'tensor'), may hold values from -0.25 to 0.25
- right_basis: float32 [32, 2048, 512], P('shard', 'tensor'), may hold values from -0.25 to 0.25
Outputs:
- update: bfloat16 [16384, 2048], P('shard', 'tensor')
- new_moment: float32 [32, 2048, 512], P('shard', 'tensor')
- new_second: float32 [32, 2048, 512], P('shard', 'tensor')
- new_left_stats: float32 [32, 2048, 512], P('shard', 'tensor')
- new_right_stats: float32 [32, 2048, 512], P('shard', 'tensor')
- new_left_basis: float32 [32, 2048, 512], P('shard', 'tensor')
- new_right_basis: float32 [32, 2048, 512], P('shard', 'tensor')
Inputs may be any that keep to these rules, and one draw needn't show every extreme that they name: `assignment`: within each block column the slots are distinct; slot a lies on index a // 1 of shard as its slot a % 1; in every block column some index of shard holds 1 block. `left_stats`: statistics carried from earlier steps. `right_stats`: statistics carried from earlier steps.
All inputs are finite; a program needn't handle non-finite values.
Results may differ from a plain program's by a relative error of at most 0.0004.
Values may be sent and summed in bfloat16 or wider, within the bound.
No kernel may reach another device: no remote copies, remote signals or barrier semaphores. Data moves between devices by JAX's collectives and lax.ppermute only.
A program may use at most 128 MiB of HBM per device.

v0:
```python
import functools
import jax
import jax.numpy as jnp
from jax import lax
from jax.experimental import pallas as pl
from jax.experimental.pallas import tpu as pltpu
from jax.sharding import PartitionSpec as P


NS_ITERS = 2
BETA_MOMENT = 0.9
BETA_SECOND = 0.9
BETA_STATS = 0.9
ADAM_EPSILON = 1e-08
CLIP_RMS = 1.0
QUINTIC_A = 3.4445
QUINTIC_B = -4.775
QUINTIC_C = 2.0315
F32, BF16 = jnp.float32, jnp.bfloat16
NN = (((1,), (0,)), ((), ()))
NT = (((1,), (1,)), ((), ()))
BLK = 256


def mxu(a, b, dims=NN):
    return lax.dot_general(a, b, dims, preferred_element_type=F32)


def split(x):
    high = x.astype(BF16)
    return high, (x - high.astype(F32)).astype(BF16)


def store_split(x, high_ref, low_ref, at=slice(None)):
    high, low = split(x)
    high_ref[at, :] = high
    low_ref[at, :] = low


def blocks(ref, n=None):
    n = ref.shape[0]
    return [pl.ds(i, BLK) for i in range(0, n, BLK)]


def prod3(ah, al, bh, bl, at, dims=NN):
    a_high = ah[at, :]
    return mxu(a_high, bh[...], dims) + (mxu(a_high, bl[...], dims) + mxu(al[at, :], bh[...], dims))


def basis_kernel(stats_ref, basis_ref, out_ref, ah, al, bh, bl, xh, xl, gh, gl, y):
    store_split(stats_ref[...], ah, al)
    store_split(basis_ref[...], bh, bl)
    total = jnp.zeros((), F32)
    for at in blocks(stats_ref):
        part = prod3(ah, al, bh, bl, at)
        y[at, :] = part
        total = total + jnp.sum(part * part)
    scale = lax.rsqrt(total + 1e-12)
    y[...] = (y[...] * scale).T
    for _ in range(NS_ITERS):
        store_split(y[...], xh, xl)
        for at in blocks(y):
            store_split(prod3(xh, xl, xh, xl, at, NT), gh, gl, at)
        for at in blocks(y):
            square = prod3(gh, gl, gh, gl, at)
            gram = gh[at, :].astype(F32) + gl[at, :].astype(F32)
            store_split(QUINTIC_B * gram + QUINTIC_C * square, ah, al, at)
        for at in blocks(y):
            y[at, :] = QUINTIC_A * y[at, :] + prod3(ah, al, xh, xl, at)
    out_ref[...] = y[...].T


def basis_call(stats, basis):
    n = stats.shape[0]
    return pl.pallas_call(
        basis_kernel,
        out_shape=jax.ShapeDtypeStruct((n, n), F32),
        in_specs=[pl.BlockSpec(memory_space=pltpu.VMEM)] * 2,
        out_specs=pl.BlockSpec(memory_space=pltpu.VMEM),
        scratch_shapes=[pltpu.VMEM((n, n), BF16)] * 8 + [pltpu.VMEM((n, n), F32)],
        compiler_params=pltpu.CompilerParams(vmem_limit_bytes=24 << 20),
        cost_estimate=pl.CostEstimate(flops=2 * n**3 * 21, bytes_accessed=3 << 20, transcendentals=0),
        name="basis",
    )(stats, basis)


def moment_kernel(left_ref, right_ref, moment_ref, out_ref, lth, ltl, lh, ll, rh, rl, mh, ml):
    left = left_ref[...]
    store_split(left, lh, ll)
    store_split(left.T, lth, ltl)
    store_split(right_ref[...], rh, rl)
    store_split(moment_ref[...], mh, ml)
    for at in blocks(left_ref):
        high, low = split(prod3(lth, ltl, mh, ml, at))
        out_ref[at, :] = mxu(high, rh[...]) + (mxu(high, rl[...]) + mxu(low, rh[...]))


def moment_call(left, right, moment):
    n = left.shape[0]
    half = jax.ShapeDtypeStruct((n, n), BF16)
    return pl.pallas_call(
        moment_kernel,
        out_shape=(jax.ShapeDtypeStruct((n, n), F32),) + (half,) * 6,
        in_specs=[pl.BlockSpec(memory_space=pltpu.VMEM)] * 3,
        out_specs=[pl.BlockSpec(memory_space=pltpu.VMEM)] * 7,
        scratch_shapes=[pltpu.VMEM((n, n), BF16)] * 2,
        compiler_params=pltpu.CompilerParams(vmem_limit_bytes=65_600_000),
        cost_estimate=pl.CostEstimate(flops=2 * n**3 * 6, bytes_accessed=7 << 20, transcendentals=0),
        name="turn",
    )(left, right, moment)


def step_kernel(entries, got_hbm, lth_hbm, ltl_hbm, rh_hbm, rl_hbm, second_hbm, pmq_hbm, lh_hbm, ll_hbm,
                update_hbm, second_out_hbm, factor_ref,
                tile_ref, sums_ref, lth, ltl, rh, rl, second_ref, pmq_ref, lh, ll, dh, dl, update_ref,
                in_sems, out_sems):
    pieces, rows = update_ref.shape[0], update_ref.shape[1]
    n = pieces * rows
    sources = (got_hbm.at[:, pl.ds(0, rows), :], lth_hbm, ltl_hbm, got_hbm.at[:, pl.ds(rows, 8), pl.ds(0, 128)],
               rh_hbm, rl_hbm, second_hbm, pmq_hbm, lh_hbm, ll_hbm)
    targets = (tile_ref, lth, ltl, sums_ref, rh, rl, second_ref, pmq_ref, lh, ll)
    loads = [
        pltpu.make_async_copy(source, target, in_sems.at[i])
        for i, (source, target) in enumerate(zip(sources, targets))
    ]
    for load in loads:
        load.start()
    for load in loads[:3]:
        load.wait()
    tile = tile_ref[...].reshape(n, n)
    for i, at in enumerate(blocks(lth)):
        high, low = split(mxu(lth[at, :], tile) + mxu(ltl[at, :], tile))
        if i == 0:
            for load in loads[3:6]:
                load.wait()
            packed = jnp.sum(sums_ref[...].astype(F32), axis=0)
            energy = packed[0:1, 0:1] + packed[1:2, 0:1] + packed[2:3, 0:1]
            factor = jnp.minimum(1.0, CLIP_RMS / jnp.sqrt(energy / entries + 1e-12))
            factor_ref[...] = jnp.broadcast_to(factor, factor_ref.shape)
        turned = mxu(high, rh[...]) + (mxu(high, rl[...]) + mxu(low, rh[...]))
        if i == 0:
            for load in loads[6:8]:
                load.wait()
        rotated = factor * turned
        second = BETA_SECOND * second_ref[at, :] + (1.0 - BETA_SECOND) * rotated * rotated
        second_ref[at, :] = second
        rotated_moment = BETA_MOMENT * pmq_ref[at, :] + (1.0 - BETA_MOMENT) * rotated
        store_split(rotated_moment / (jnp.sqrt(second) + ADAM_EPSILON), dh, dl, at)
    for load in loads[8:]:
        load.wait()
    count = BLK // rows
    stores = []
    for i, at in enumerate(blocks(lth)):
        high, low = split(prod3(lh, ll, dh, dl, at))
        if i == 0:
            stores.append(pltpu.make_async_copy(second_ref, second_out_hbm, out_sems.at[0]))
            stores[-1].start()
        out = mxu(high, rh[...], NT) + (mxu(high, rl[...], NT) + mxu(low, rh[...], NT))
        if i > 0:
            stores.append(send_rows(update_ref, update_hbm, i - 1, count, out_sems))
        update_ref[i * count : (i + 1) * count] = out.astype(BF16).reshape(count, rows, n)
    stores.append(send_rows(update_ref, update_hbm, n // BLK - 1, count, out_sems))
    for store in stores:
        store.wait()


def send_rows(source, target, i, count, sems):
    part = pl.ds(i * count, count)
    copy = pltpu.make_async_copy(source.at[part], target.at[part], sems.at[i + 1])
    copy.start()
    return copy


def step_call(entries, got, halves, pmq, second):
    n = pmq.shape[0]
    pieces = got.shape[0]
    lth, ltl, lh, ll, rh, rl = halves
    half, full = pltpu.VMEM((n, n), BF16), pltpu.VMEM((n, n), F32)
    hbm = pl.BlockSpec(memory_space=pltpu.HBM)
    vmem = pl.BlockSpec(memory_space=pltpu.VMEM)
    block = pltpu.VMEM((pieces, n // pieces, n), BF16)
    return pl.pallas_call(
        functools.partial(step_kernel, entries),
        out_shape=(
            jax.ShapeDtypeStruct((pieces, n // pieces, n), BF16),
            jax.ShapeDtypeStruct((n, n), F32),
            jax.ShapeDtypeStruct((8, 128), F32),
        ),
        in_specs=[hbm] * 9,
        out_specs=[hbm, hbm, vmem],
        scratch_shapes=[block, pltpu.VMEM((pieces, 8, 128), BF16)]
        + [half] * 4
        + [full] * 2
        + [half] * 4
        + [block, pltpu.SemaphoreType.DMA((10,)), pltpu.SemaphoreType.DMA((n // BLK + 1,))],
        compiler_params=pltpu.CompilerParams(vmem_limit_bytes=66_500_000),
        cost_estimate=pl.CostEstimate(flops=2 * n**3 * 11, bytes_accessed=7 << 20, transcendentals=0),
        name="step",
    )(got, lth, ltl, rh, rl, second, pmq, lh, ll)


def state_kernel(got_ref, factor_ref, moment_ref, left_ref, right_ref, moment_out, left_out, right_out):
    n = moment_ref.shape[0]
    rows = n // got_ref.shape[0]
    tile = got_ref[:, :rows, :].reshape(n, n)
    factor = factor_ref[0:1, 0:1]
    scale = (1.0 - BETA_STATS) * factor * factor / n
    turned = tile.T
    for at in blocks(moment_ref):
        mine = tile[at.start : at.start + BLK, :]
        moment_out[at, :] = BETA_MOMENT * moment_ref[at, :] + (1.0 - BETA_MOMENT) * (factor * mine.astype(F32))
        left_out[at, :] = BETA_STATS * left_ref[at, :] + scale * mxu(mine, tile, NT)
        right_out[at, :] = BETA_STATS * right_ref[at, :] + scale * mxu(turned[at.start : at.start + BLK, :], tile)


def state_call(got, factor, moment, left, right):
    n = moment.shape[0]
    full = jax.ShapeDtypeStruct((n, n), F32)
    return pl.pallas_call(
        state_kernel,
        out_shape=(full,) * 3,
        in_specs=[pl.BlockSpec(memory_space=pltpu.VMEM)] * 5,
        out_specs=[pl.BlockSpec(memory_space=pltpu.VMEM)] * 3,
        compiler_params=pltpu.CompilerParams(vmem_limit_bytes=16 << 20),
        cost_estimate=pl.CostEstimate(flops=2 * n**3 * 2, bytes_accessed=7 << 20, transcendentals=0),
        name="state",
    )(got, factor, moment, left, right)


def energy_kernel(grads_ref, out_ref):
    x = grads_ref[...].astype(F32)
    out_ref[...] = jnp.full(out_ref.shape, jnp.sum(x * x))


def energy_call(grads):
    return pl.pallas_call(
        energy_kernel,
        out_shape=jax.ShapeDtypeStruct((8, 128), F32),
        in_specs=[pl.BlockSpec(memory_space=pltpu.VMEM)],
        out_specs=pl.BlockSpec(memory_space=pltpu.VMEM),
        compiler_params=pltpu.CompilerParams(vmem_limit_bytes=4 << 20),
        cost_estimate=pl.CostEstimate(flops=1 << 19, bytes_accessed=1 << 19, transcendentals=0),
        name="energy",
    )(grads)


def route_kernel(slots_ref, own_ref, other_ref, energy_ref, out_ref, source_ref):
    chips, rows = own_ref.shape[0], own_ref.shape[1]
    core = lax.rem(lax.axis_index("shard"), 2)
    for i in range(2 * chips):
        source_ref[slots_ref[0, i]] = i
    energy = energy_ref[...]
    high = energy.astype(BF16).astype(F32)
    middle = (energy - high).astype(BF16).astype(F32)
    low = energy - high - middle
    row = lax.broadcasted_iota(jnp.int32, energy.shape, 0)
    packed = jnp.where(row == 0, high, jnp.where(row == 1, middle, low)).astype(BF16)
    packed = jnp.concatenate([packed] * (out_ref.shape[2] // 128), axis=1)
    for chip in range(chips):
        block = source_ref[2 * chip + core]
        mine = lax.rem(block, 2) == core
        out_ref[chip, :rows, :] = jnp.where(mine, own_ref[block // 2], other_ref[block // 2])
        out_ref[chip, rows:, :] = packed


def return_kernel(slots_ref, own_ref, other_ref, out_ref):
    core = lax.rem(lax.axis_index("shard"), 2)
    for i in range(own_ref.shape[0]):
        slot = slots_ref[0, 2 * i + core]
        mine = lax.rem(slot, 2) == core
        out_ref[i] = jnp.where(mine, own_ref[slot // 2], other_ref[slot // 2])


def pick_call(kernel, rows, scratch, operands):
    chips, size = operands[1].shape[0], operands[1].shape[2]
    return pl.pallas_call(
        kernel,
        out_shape=jax.ShapeDtypeStruct((chips, rows, size), BF16),
        in_specs=[pl.BlockSpec(memory_space=pltpu.SMEM)]
        + [pl.BlockSpec(memory_space=pltpu.VMEM)] * (len(operands) - 1),
        out_specs=pl.BlockSpec(memory_space=pltpu.VMEM),
        scratch_shapes=scratch,
        compiler_params=pltpu.CompilerParams(vmem_limit_bytes=8 << 20),
        cost_estimate=pl.CostEstimate(flops=0, bytes_accessed=1 << 21, transcendentals=0),
    )(*operands)


def shards(grads, assignment, moment, second, left_stats, right_stats, left_basis, right_basis):
    shard_count = lax.axis_size("shard")
    tensor_count = lax.axis_size("tensor")
    size = grads.shape[1]
    chips = shard_count // 2
    rows = size // chips
    entries = float(size * size * shard_count * tensor_count)
    same_core = [[2 * p + q for p in range(chips)] for q in range(2)]
    swap = [(i, i ^ 1) for i in range(shard_count)]
    moment, second = moment[0], second[0]
    left_stats, right_stats = left_stats[0], right_stats[0]
    left_basis, right_basis = left_basis[0], right_basis[0]

    def exchange(pieces):
        return lax.all_to_all(pieces, "shard", 0, 0, axis_index_groups=same_core)

    arrived = exchange(grads.reshape(chips, rows, size))
    energy = energy_call(grads)
    moved = [
        lax.ppermute(
            energy, "tensor", [(i, (i + s) % tensor_count) for i in range(tensor_count)]
        )
        for s in range(1, tensor_count)
    ]
    turned, *halves = moment_call(left_basis, right_basis, moment)
    moved, turned = lax.optimization_barrier((moved, turned))
    for part in moved:
        energy = energy + part
    energy = energy + lax.ppermute(energy, "shard", swap)
    other = lax.ppermute(arrived, "shard", swap)
    routed = pick_call(
        route_kernel, rows + 8, [pltpu.SMEM((shard_count,), jnp.int32)], (assignment, arrived, other, energy)
    )
    got = exchange(routed)
    left_basis_new = basis_call(left_stats, left_basis)
    update, second_new, factor = step_call(entries, got, halves, turned, second)
    returned = exchange(update)
    right_basis_new = basis_call(right_stats, right_basis)
    other = lax.ppermute(returned, "shard", swap)
    picked = pick_call(return_kernel, rows, [], (assignment, returned, other))
    update_out = exchange(picked).reshape(size, size)
    moment_new, left_new, right_new = state_call(got, factor, moment, left_stats, right_stats)

    states = (moment_new, second_new, left_new, right_new, left_basis_new, right_basis_new)
    return (update_out,) + tuple(state[None] for state in states)


def solution(mesh):
    weights = P("shard", "tensor")
    state = P("shard", "tensor", None)

    return jax.shard_map(
        shards,
        mesh=mesh,
        in_specs=(weights, P("tensor", None)) + (state,) * 6,
        out_specs=(weights,) + (state,) * 6,
        check_vma=False,
    )
```

profile of v0, /device:TPU:0, one launch (start us, length us, event | category | flops | bytes accessed | tf_op | source)
XLA Modules:
  0.0 101.5 jit_solution(5928769578803351037)
XLA Ops:
  0.6 0.0 copy-start.1
  0.6 18.8 %all_to_all.20.own_ref = bf16[16,32,512]{2,1,0:T(8,128)(2,1)S(1)} all-to-all(bf16[16,32,512]{2,1,0:T(8,128)(2,1)} %bitcast.14), channel_id=1, replica_groups={{0,8,16,24,32,40,48,56,64,72,80,88,96,104,112,120},{4,12,20,28,36,44,52..., dimensions={0} | all-to-all | bytes 1048576 | tf_op jit(solution)/shard_map/all_to_all | solution.py:302
  19.5 0.0 collective-permute-start
  19.5 0.0 copy-done.1
  19.5 0.4 energy.1
  19.9 2.0 %collective-permute-start.1 = (f32[8,128]{1,0:T(8,128)S(1)}, f32[8,128]{1,0:T(8,128)S(1)}, u32[]{:S(2)}, u32[]{:S(2)}) collective-permute-start(f32[8,128]{1,0:T(8,128)S(1)} %energy.1), channel_id=1, source_target_pairs={{0,1},{1,2},{2,3},{3,0},{4,5},{5,6},{6,7},{7,4},{8,9},{9,10},{10,1... | collective-permute-start | bytes 12296 | tf_op jit(solution)/shard_map/ppermute | solution.py:307
  21.9 3.6 %collective-permute-start.2 = (f32[8,128]{1,0:T(8,128)S(1)}, f32[8,128]{1,0:T(8,128)S(1)}, u32[]{:S(2)}, u32[]{:S(2)}) collective-permute-start(f32[8,128]{1,0:T(8,128)S(1)} %energy.1), channel_id=1, source_target_pairs={{0,2},{1,3},{2,0},{3,1},{4,6},{5,7},{6,4},{7,5},{8,10},{9,11},{10,... | collective-permute-start | bytes 12296 | tf_op jit(solution)/shard_map/ppermute | solution.py:307
  25.4 1.0 collective-permute-start.3
  26.4 4.9 %turn.1 = (f32[512,512]{1,0:T(8,128)}, bf16[512,512]{1,0:T(8,128)(2,1)}, bf16[512,512]{1,0:T(8,128)(2,1)}, bf16[512,512]{1,0:T(8,128)(2,1)}, bf16[512,512]{1,0:T...) custom-call(f32[512,512]{1,0:T(8,128)} %bitcast.21, f32[512,512]{1,0:T(8,128)} %bitcast.23, ...), custom_call_target="tpu_custom_call" | custom-call | flops 1610612736 | bytes 7340032 | tf_op jit(solution)/shard_map/turn/pallas_call | solution.py:101
  31.3 0.0 collective-permute-done.1
  31.3 0.0 collective-permute-done.2
  31.4 0.0 collective-permute-done.3
  31.4 0.0 copy-start.6
  31.4 0.1 collective-permute-start.4
  31.5 1.2 %collective-permute-done.4 = f32[8,128]{1,0:T(8,128)S(1)} collective-permute-done((f32[8,128]{1,0:T(8,128)S(1)}, f32[8,128]{1,0:T(8,128)S(1)}, u32[]{:S(2)}, u32[]{:S(2)}) %collective-permute-start.4) | collective-permute-done | bytes 4128 | tf_op jit(solution)/shard_map/ppermute | solution.py:316
  32.6 0.0 collective-permute-done.other_ref
  32.6 0.0 copy-done.6
  32.7 0.7 shard_map.135
  33.4 16.8 %all_to_all.21.got_hbm.got_ref = bf16[16,40,512]{2,1,0:T(8,128)(2,1)} all-to-all(bf16[16,40,512]{2,1,0:T(8,128)(2,1)S(1)} %shard_map.135), channel_id=1, replica_groups={{0,8,16,24,32,40,48,56,64,72,80,88,96,104,112,120},{4,12,20,28,36,44,52..., dimensions={0} | all-to-all | bytes 1310720 | tf_op jit(solution)/shard_map/all_to_all | solution.py:302
  50.2 7.3 %step.1 = (bf16[16,32,512]{2,1,0:T(8,128)(2,1)}, f32[512,512]{1,0:T(8,128)}, f32[8,128]{1,0:T(8,128)}) custom-call(bf16[16,40,512]{2,1,0:T(8,128)(2,1)} %all_to_all.21.got_hbm.got_ref, bf16[512,512]{1,0:T(8,128)(2,1)} %get-tuple-element.28.lth_hbm, bf16[512,512]{1,0:T(8,128)(2,1)} %get-tuple-element.29.ltl_hbm, bf16[512,512]{1,0:T(8,128)(2,1)} %get-tuple-element.30.rh_hbm, ...), custom_call_target="tpu_custom_call" | custom-call | flops 2952790016 | bytes 7340032 | tf_op jit(solution)/shard_map/step/pallas_call | solution.py:182
  57.5 0.0 copy-start.3
  57.5 15.0 %all_to_all.22.own_ref = bf16[16,32,512]{2,1,0:T(8,128)(2,1)S(1)} all-to-all(bf16[16,32,512]{2,1,0:T(8,128)(2,1)} %get-tuple-element.35), channel_id=1, replica_groups={{0,8,16,24,32,40,48,56,64,72,80,88,96,104,112,120},{4,12,20,28,36,44,52..., dimensions={0} | all-to-all | bytes 1048576 | tf_op jit(solution)/shard_map/all_to_all | solution.py:302
  72.5 0.0 collective-permute-start.5
  72.5 0.0 copy-done.3
  72.5 0.0 copy-start.7
  72.5 1.2 %copy-done.7 = f32[1,512,512]{2,1,0:T(8,128)S(1)} copy-done((f32[1,512,512]{2,1,0:T(8,128)S(1)}, f32[1,512,512]{2,1,0:T(8,128)}, u32[]{:S(2)}) %copy-start.7) | copy-done | bytes 1048600
  73.7 7.7 %basis.2 = f32[512,512]{1,0:T(8,128)} custom-call(f32[512,512]{1,0:T(8,128)S(1)} %bitcast.17, f32[512,512]{1,0:T(8,128)S(1)} %bitcast.22), custom_call_target="tpu_custom_call" | custom-call | flops 5637144576 | bytes 3145728 | tf_op jit(solution)/shard_map/basis/pallas_call | solution.py:75
  81.4 0.0 copy-start.4
  81.4 0.0 copy-start.8
  81.4 0.0 collective-permute-done.5.other_ref
  81.4 1.5 %shard_map.136 = bf16[16,32,512]{2,1,0:T(8,128)(2,1)} custom-call(s32[1,32]{1,0:T(1,128)S(1)} %copy-done.6, bf16[16,32,512]{2,1,0:T(8,128)(2,1)S(1)} %all_to_all.22.own_ref, bf16[16,32,512]{2,1,0:T(8,128)(2,1)S(1)} %collective-permute-done.5.other_ref), custom_call_target="tpu_custom_call" | custom-call | bytes 2097152 | tf_op jit(solution)/shard_map/pallas_call | solution.py:276
  82.9 4.5 %all-to-all-start.3 = ((bf16[16,32,512]{2,1,0:T(8,128)(2,1)}), bf16[16,32,512]{2,1,0:T(8,128)(2,1)}, u32[]{:S(2)}, u32[]{:S(2)}) async-start(bf16[16,32,512]{2,1,0:T(8,128)(2,1)} %shard_map.136), calls=%async_computation.3 | async-start | bytes 1048576 | tf_op jit(solution)/shard_map/all_to_all | solution.py:302
  87.4 0.0 copy-done.4
  87.4 0.0 copy-done.8
  87.4 0.0 copy-start
  87.4 0.0 copy-start.2
  87.4 0.0 copy-start.5
  87.4 7.7 %basis.3 = f32[512,512]{1,0:T(8,128)} custom-call(f32[512,512]{1,0:T(8,128)S(1)} %bitcast.19, f32[512,512]{1,0:T(8,128)S(1)} %bitcast.24), custom_call_target="tpu_custom_call" | custom-call | flops 5637144576 | bytes 3145728 | tf_op jit(solution)/shard_map/basis/pallas_call | solution.py:75
  95.2 0.0 copy-done
  95.2 0.0 copy-done.2
  95.2 0.0 copy-done.5
  95.2 2.3 %state.1 = (f32[512,512]{1,0:T(8,128)}, f32[512,512]{1,0:T(8,128)}, f32[512,512]{1,0:T(8,128)}) custom-call(bf16[16,40,512]{2,1,0:T(8,128)(2,1)S(1)} %copy-done, f32[8,128]{1,0:T(8,128)S(1)} %copy-done.5, f32[512,512]{1,0:T(8,128)S(1)} %bitcast.16, f32[512,512]{1,0:T(8,128)S(1)} %bitcast.18, f32[512,512]{1,0:T(8,128)S(1)} %bitcast.20), custom_call_target="tpu_custom_call" | custom-call | flops 536870912 | bytes 7340032 | tf_op jit(solution)/shard_map/state/pallas_call | solution.py:219
  97.4 2.2 %all-to-all-done.3 = bf16[16,32,512]{2,1,0:T(8,128)(2,1)} async-done(((bf16[16,32,512]{2,1,0:T(8,128)(2,1)}), bf16[16,32,512]{2,1,0:T(8,128)(2,1)}, u32[]{:S(2)}, u32[]{:S(2)}) %all-to-all-start.3) | async-done | bytes 524320 | tf_op jit(solution)/shard_map/all_to_all | solution.py:302
  99.6 1.9 %copy.16 = bf16[512,512]{1,0:T(8,128)(2,1)} copy(bf16[512,512]{1,0:T(8,128)(2,1)} %bitcast.5) | data formatting | bytes 1048576
  (2 shorter events, 0.0 us)
Async XLA Ops:
  0.6 18.8 %copy-start.1 = (bf16[512,512]{1,0:T(8,128)(2,1)S(1)}, bf16[512,512]{1,0:T(8,128)(2,1)}, u32[]{:S(2)}) copy-start(bf16[512,512]{1,0:T(8,128)(2,1)} %grads_ref.1) | copy-start | bytes 1572868
  19.5 13.2 %collective-permute-start = (bf16[16,32,512]{2,1,0:T(8,128)(2,1)S(1)}, bf16[16,32,512]{2,1,0:T(8,128)(2,1)S(1)}, u32[]{:S(2)}, u32[]{:S(2)}) collective-permute-start(bf16[16,32,512]{2,1,0:T(8,128)(2,1)S(1)} %all_to_all.20.own_ref), channel_id=1, source_target_pairs={{0,4},{4,0},{8,12},{12,8},{16,20},{20,16},{24,28},{28,24},{32,36},... | collective-permute-start | bytes 1572872 | tf_op jit(solution)/shard_map/ppermute | solution.py:317
  19.9 11.5 %collective-permute-start.1 = (f32[8,128]{1,0:T(8,128)S(1)}, f32[8,128]{1,0:T(8,128)S(1)}, u32[]{:S(2)}, u32[]{:S(2)}) collective-permute-start(f32[8,128]{1,0:T(8,128)S(1)} %energy.1), channel_id=1, source_target_pairs={{0,1},{1,2},{2,3},{3,0},{4,5},{5,6},{6,7},{7,4},{8,9},{9,10},{10,1... | collective-permute-start | bytes 12296 | tf_op jit(solution)/shard_map/ppermute | solution.py:307
  21.9 9.5 %collective-permute-start.2 = (f32[8,128]{1,0:T(8,128)S(1)}, f32[8,128]{1,0:T(8,128)S(1)}, u32[]{:S(2)}, u32[]{:S(2)}) collective-permute-start(f32[8,128]{1,0:T(8,128)S(1)} %energy.1), channel_id=1, source_target_pairs={{0,2},{1,3},{2,0},{3,1},{4,6},{5,7},{6,4},{7,5},{8,10},{9,11},{10,... | collective-permute-start | bytes 12296 | tf_op jit(solution)/shard_map/ppermute | solution.py:307
  25.4 5.9 %collective-permute-start.3 = (f32[8,128]{1,0:T(8,128)S(1)}, f32[8,128]{1,0:T(8,128)S(1)}, u32[]{:S(2)}, u32[]{:S(2)}) collective-permute-start(f32[8,128]{1,0:T(8,128)S(1)} %energy.1), channel_id=1, source_target_pairs={{0,3},{1,0},{2,1},{3,2},{4,7},{5,4},{6,5},{7,6},{8,11},{9,8},{10,9... | collective-permute-start | bytes 12296 | tf_op jit(solution)/shard_map/ppermute | solution.py:307
  31.4 1.3 %copy-start.6 = (s32[1,32]{1,0:T(1,128)S(1)}, s32[1,32]{1,0:T(1,128)}, u32[]{:S(2)}) copy-start(s32[1,32]{1,0:T(1,128)} %slots_ref.3) | copy-start | bytes 388
  31.4 1.2 %collective-permute-start.4 = (f32[8,128]{1,0:T(8,128)S(1)}, f32[8,128]{1,0:T(8,128)S(1)}, u32[]{:S(2)}, u32[]{:S(2)}) collective-permute-start(f32[8,128]{1,0:T(8,128)S(1)} %add_add_fusion), channel_id=1, source_target_pairs={{0,4},{4,0},{8,12},{12,8},{16,20},{20,16},{24,28},{28,24},{32,36},... | collective-permute-start | bytes 12296 | tf_op jit(solution)/shard_map/ppermute | solution.py:316
  57.5 15.0 %copy-start.3 = (f32[1,512,512]{2,1,0:T(8,128)S(1)}, f32[1,512,512]{2,1,0:T(8,128)}, u32[]{:S(2)}) copy-start(f32[1,512,512]{2,1,0:T(8,128)} %param.12) | copy-start | bytes 3145732
  72.5 9.0 %collective-permute-start.5 = (bf16[16,32,512]{2,1,0:T(8,128)(2,1)S(1)}, bf16[16,32,512]{2,1,0:T(8,128)(2,1)S(1)}, u32[]{:S(2)}, u32[]{:S(2)}) collective-permute-start(bf16[16,32,512]{2,1,0:T(8,128)(2,1)S(1)} %all_to_all.22.own_ref), channel_id=1, source_target_pairs={{0,4},{4,0},{8,12},{12,8},{16,20},{20,16},{24,28},{28,24},{32,36},... | collective-permute-start | bytes 1572872 | tf_op jit(solution)/shard_map/ppermute | solution.py:326
  72.5 1.2 %copy-start.7 = (f32[1,512,512]{2,1,0:T(8,128)S(1)}, f32[1,512,512]{2,1,0:T(8,128)}, u32[]{:S(2)}) copy-start(f32[1,512,512]{2,1,0:T(8,128)} %param.14) | copy-start | bytes 3145732
  81.4 5.9 %copy-start.4 = (f32[1,512,512]{2,1,0:T(8,128)S(1)}, f32[1,512,512]{2,1,0:T(8,128)}, u32[]{:S(2)}) copy-start(f32[1,512,512]{2,1,0:T(8,128)} %param.13) | copy-start | bytes 3145732
  81.4 6.0 %copy-start.8 = (f32[1,512,512]{2,1,0:T(8,128)S(1)}, f32[1,512,512]{2,1,0:T(8,128)}, u32[]{:S(2)}) copy-start(f32[1,512,512]{2,1,0:T(8,128)} %param.15) | copy-start | bytes 3145732
  82.9 16.7 %all-to-all-start.3 = ((bf16[16,32,512]{2,1,0:T(8,128)(2,1)}), bf16[16,32,512]{2,1,0:T(8,128)(2,1)}, u32[]{:S(2)}, u32[]{:S(2)}) async-start(bf16[16,32,512]{2,1,0:T(8,128)(2,1)} %shard_map.136), calls=%async_computation.3 | async-start | bytes 1048576 | tf_op jit(solution)/shard_map/all_to_all | solution.py:302
  87.4 7.8 %copy-start = (bf16[16,40,512]{2,1,0:T(8,128)(2,1)S(1)}, bf16[16,40,512]{2,1,0:T(8,128)(2,1)}, u32[]{:S(2)}) copy-start(bf16[16,40,512]{2,1,0:T(8,128)(2,1)} %all_to_all.21.got_hbm.got_ref) | copy-start | bytes 1966084
  87.4 7.8 %copy-start.2 = (f32[1,512,512]{2,1,0:T(8,128)S(1)}, f32[1,512,512]{2,1,0:T(8,128)}, u32[]{:S(2)}) copy-start(f32[1,512,512]{2,1,0:T(8,128)} %param.10) | copy-start | bytes 3145732
  87.4 7.7 %copy-start.5 = (f32[8,128]{1,0:T(8,128)S(1)}, f32[8,128]{1,0:T(8,128)}, u32[]{:S(2)}) copy-start(f32[8,128]{1,0:T(8,128)} %get-tuple-element.36.factor_ref) | copy-start | bytes 12292
where the time goes:
time: 102 us
  blocking collectives  50.6 us (50%)
  Pallas kernels  32.5 us (32%)
  starting transfers between devices  11.1 us (11%)
  waiting for transfers between devices  3.38 us (3%)
  local copies, waits for them, and re-layouts  3.13 us (3%)
    all_to_all x3, blocking collectives, exchange(): return lax.all_to_all(pieces, 'shard', 0, 0, axis_index_groups=same_core)  50.6 us
    pallas_call x2, Pallas kernels, basis_call(): pl.pallas_call(basis_kernel, out_shape=jax.ShapeDtypeStruct((n, n), F32),...  15.5 us
    pallas_call x1, Pallas kernels, step_call(): pl.pallas_call(functools.partial(step_kernel, entries), out_shape=(jax.Sh...  7.3 us
    ppermute x3, starting transfers between devices, shards(): lax.ppermute(energy, 'tensor', [(i, (i + s) % tensor_count) for i in rang...  6.58 us
    pallas_call x1, Pallas kernels, moment_call(): pl.pallas_call(moment_kernel, out_shape=(jax.ShapeDtypeStruct((n, n), F32...  4.9 us
    all_to_all x1, starting transfers between devices, exchange(): return lax.all_to_all(pieces, 'shard', 0, 0, axis_index_groups=same_core)  4.47 us
    unnamed x19, local copies, waits for them, and re-layouts  3.13 us
    pallas_call x1, Pallas kernels, state_call(): pl.pallas_call(state_kernel, out_shape=(full,) * 3, in_specs=[pl.BlockSpe...  2.27 us
  transfers between devices with their start and end apart: 7, of which 2 were waited for; matrix products, arithmetic and copies ran while one was open for 0% of the time, Pallas kernels for 23%

commit v1 on v0

--- a/solution.py
+++ b/solution.py
@@ -47,41 +47,60 @@
     return mxu(a_high, bh[...], dims) + (mxu(a_high, bl[...], dims) + mxu(al[at, :], bh[...], dims))
 
 
-def basis_kernel(stats_ref, basis_ref, out_ref, ah, al, bh, bl, xh, xl, gh, gl, y):
+def sweep(y, ah, al, xh, xl, gh, gl):
+    store_split(y[...], xh, xl)
+    for at in blocks(y):
+        store_split(prod3(xh, xl, xh, xl, at, NT), gh, gl, at)
+    for at in blocks(y):
+        square = prod3(gh, gl, gh, gl, at)
+        gram = gh[at, :].astype(F32) + gl[at, :].astype(F32)
+        store_split(QUINTIC_B * gram + QUINTIC_C * square, ah, al, at)
+    for at in blocks(y):
+        y[at, :] = QUINTIC_A * y[at, :] + prod3(ah, al, xh, xl, at)
+
+
+def open_kernel(sweeps, stats_ref, basis_ref, y, ah, al, xh, xl, gh, gl):
     store_split(stats_ref[...], ah, al)
-    store_split(basis_ref[...], bh, bl)
+    store_split(basis_ref[...], xh, xl)
     total = jnp.zeros((), F32)
     for at in blocks(stats_ref):
-        part = prod3(ah, al, bh, bl, at)
+        part = prod3(ah, al, xh, xl, at)
         y[at, :] = part
         total = total + jnp.sum(part * part)
     scale = lax.rsqrt(total + 1e-12)
     y[...] = (y[...] * scale).T
-    for _ in range(NS_ITERS):
-        store_split(y[...], xh, xl)
-        for at in blocks(y):
-            store_split(prod3(xh, xl, xh, xl, at, NT), gh, gl, at)
-        for at in blocks(y):
-            square = prod3(gh, gl, gh, gl, at)
-            gram = gh[at, :].astype(F32) + gl[at, :].astype(F32)
-            store_split(QUINTIC_B * gram + QUINTIC_C * square, ah, al, at)
-        for at in blocks(y):
-            y[at, :] = QUINTIC_A * y[at, :] + prod3(ah, al, xh, xl, at)
+    for _ in range(sweeps):
+        sweep(y, ah, al, xh, xl, gh, gl)
+    if sweeps == NS_ITERS:
+        y[...] = y[...].T
+
+
+def close_kernel(sweeps, start_ref, out_ref, y, ah, al, xh, xl, gh, gl):
+    y[...] = start_ref[...]
+    for _ in range(sweeps):
+        sweep(y, ah, al, xh, xl, gh, gl)
     out_ref[...] = y[...].T
 
 
-def basis_call(stats, basis):
-    n = stats.shape[0]
-    return pl.pallas_call(
-        basis_kernel,
+def basis_call(kernel, sweeps, operands, extra):
+    n = operands[0].shape[0]
+    return pl.pallas_call(
+        functools.partial(kernel, sweeps),
         out_shape=jax.ShapeDtypeStruct((n, n), F32),
-        in_specs=[pl.BlockSpec(memory_space=pltpu.VMEM)] * 2,
+        in_specs=[pl.BlockSpec(memory_space=pltpu.VMEM)] * len(operands),
         out_specs=pl.BlockSpec(memory_space=pltpu.VMEM),
-        scratch_shapes=[pltpu.VMEM((n, n), BF16)] * 8 + [pltpu.VMEM((n, n), F32)],
-        compiler_params=pltpu.CompilerParams(vmem_limit_bytes=24 << 20),
-        cost_estimate=pl.CostEstimate(flops=2 * n**3 * 21, bytes_accessed=3 << 20, transcendentals=0),
-        name="basis",
-    )(stats, basis)
+        scratch_shapes=[pltpu.VMEM((n, n), F32)] * extra + [pltpu.VMEM((n, n), BF16)] * 6,
+        compiler_params=pltpu.CompilerParams(vmem_limit_bytes=64_900_000),
+        cost_estimate=pl.CostEstimate(flops=2 * n**3 * 9 * sweeps, bytes_accessed=3 << 20, transcendentals=0),
+    )(*operands)
+
+
+def open_basis(stats, basis, sweeps):
+    return basis_call(open_kernel, sweeps, (stats, basis), 0)
+
+
+def close_basis(start, sweeps):
+    return basis_call(close_kernel, sweeps, (start,), 1)
 
 
 def moment_kernel(left_ref, right_ref, moment_ref, out_ref, lth, ltl, lh, ll, rh, rl, mh, ml):
@@ -110,43 +129,51 @@
     )(left, right, moment)
 
 
+def tiles(rows, n):
+    across = n // 128
+    return [
+        (pl.ds((high * across + wide) * 16, 16), pl.ds(high * 16, 16), pl.ds(wide * 128, 128))
+        for high in range(rows // 16)
+        for wide in range(across)
+    ]
+
+
 def step_kernel(entries, got_hbm, lth_hbm, ltl_hbm, rh_hbm, rl_hbm, second_hbm, pmq_hbm, lh_hbm, ll_hbm,
                 update_hbm, second_out_hbm, factor_ref,
-                tile_ref, sums_ref, lth, ltl, rh, rl, second_ref, pmq_ref, lh, ll, dh, dl, update_ref,
+                got_ref, tile_ref, lth, ltl, rh, rl, second_ref, pmq_ref, lh, ll, dh, dl, update_ref,
                 in_sems, out_sems):
     pieces, rows = update_ref.shape[0], update_ref.shape[1]
     n = pieces * rows
-    sources = (got_hbm.at[:, pl.ds(0, rows), :], lth_hbm, ltl_hbm, got_hbm.at[:, pl.ds(rows, 8), pl.ds(0, 128)],
-               rh_hbm, rl_hbm, second_hbm, pmq_hbm, lh_hbm, ll_hbm)
-    targets = (tile_ref, lth, ltl, sums_ref, rh, rl, second_ref, pmq_ref, lh, ll)
-    loads = [
-        pltpu.make_async_copy(source, target, in_sems.at[i])
-        for i, (source, target) in enumerate(zip(sources, targets))
-    ]
+    pairs = [(got_hbm, got_ref), (lth_hbm, lth), (ltl_hbm, ltl)]
+    pairs += [(rh_hbm, rh), (rl_hbm, rl), (second_hbm, second_ref), (pmq_hbm, pmq_ref), (lh_hbm, lh), (ll_hbm, ll)]
+    loads = [pltpu.make_async_copy(source, target, in_sems.at[i]) for i, (source, target) in enumerate(pairs)]
     for load in loads:
         load.start()
-    for load in loads[:3]:
+    loads[0].wait()
+    for part, high, wide in tiles(rows, n):
+        tile_ref[:, high, wide] = got_ref[:, part, :]
+    for load in loads[1:3]:
         load.wait()
+    packed = jnp.sum(got_ref[:, rows * n // 128 :, :].astype(F32), axis=0)
+    energy = packed[0:1, 0:1] + packed[1:2, 0:1] + packed[2:3, 0:1]
+    factor = jnp.minimum(1.0, CLIP_RMS / jnp.sqrt(energy / entries + 1e-12))
+    factor_ref[...] = jnp.broadcast_to(factor, factor_ref.shape)
     tile = tile_ref[...].reshape(n, n)
     for i, at in enumerate(blocks(lth)):
         high, low = split(mxu(lth[at, :], tile) + mxu(ltl[at, :], tile))
         if i == 0:
-            for load in loads[3:6]:
+            for load in loads[3:5]:
                 load.wait()
-            packed = jnp.sum(sums_ref[...].astype(F32), axis=0)
-            energy = packed[0:1, 0:1] + packed[1:2, 0:1] + packed[2:3, 0:1]
-            factor = jnp.minimum(1.0, CLIP_RMS / jnp.sqrt(energy / entries + 1e-12))
-            factor_ref[...] = jnp.broadcast_to(factor, factor_ref.shape)
         turned = mxu(high, rh[...]) + (mxu(high, rl[...]) + mxu(low, rh[...]))
         if i == 0:
-            for load in loads[6:8]:
+            for load in loads[5:7]:
                 load.wait()
         rotated = factor * turned
         second = BETA_SECOND * second_ref[at, :] + (1.0 - BETA_SECOND) * rotated * rotated
         second_ref[at, :] = second
         rotated_moment = BETA_MOMENT * pmq_ref[at, :] + (1.0 - BETA_MOMENT) * rotated
         store_split(rotated_moment / (jnp.sqrt(second) + ADAM_EPSILON), dh, dl, at)
-    for load in loads[8:]:
+    for load in loads[7:]:
         load.wait()
     count = BLK // rows
     stores = []
@@ -188,21 +215,23 @@
         ),
         in_specs=[hbm] * 9,
         out_specs=[hbm, hbm, vmem],
-        scratch_shapes=[block, pltpu.VMEM((pieces, 8, 128), BF16)]
+        scratch_shapes=[pltpu.VMEM(got.shape, BF16), block]
         + [half] * 4
         + [full] * 2
         + [half] * 4
-        + [block, pltpu.SemaphoreType.DMA((10,)), pltpu.SemaphoreType.DMA((n // BLK + 1,))],
+        + [block, pltpu.SemaphoreType.DMA((9,)), pltpu.SemaphoreType.DMA((n // BLK + 1,))],
         compiler_params=pltpu.CompilerParams(vmem_limit_bytes=66_500_000),
         cost_estimate=pl.CostEstimate(flops=2 * n**3 * 11, bytes_accessed=7 << 20, transcendentals=0),
         name="step",
     )(got, lth, ltl, rh, rl, second, pmq, lh, ll)
 
 
-def state_kernel(got_ref, factor_ref, moment_ref, left_ref, right_ref, moment_out, left_out, right_out):
+def state_kernel(got_ref, factor_ref, moment_ref, left_ref, right_ref, moment_out, left_out, right_out, tile_ref):
     n = moment_ref.shape[0]
-    rows = n // got_ref.shape[0]
-    tile = got_ref[:, :rows, :].reshape(n, n)
+    rows = tile_ref.shape[1]
+    for part, high, wide in tiles(rows, n):
+        tile_ref[:, high, wide] = got_ref[:, part, :]
+    tile = tile_ref[...].reshape(n, n)
     factor = factor_ref[0:1, 0:1]
     scale = (1.0 - BETA_STATS) * factor * factor / n
     turned = tile.T
@@ -221,7 +250,8 @@
         out_shape=(full,) * 3,
         in_specs=[pl.BlockSpec(memory_space=pltpu.VMEM)] * 5,
         out_specs=[pl.BlockSpec(memory_space=pltpu.VMEM)] * 3,
-        compiler_params=pltpu.CompilerParams(vmem_limit_bytes=16 << 20),
+        scratch_shapes=[pltpu.VMEM((got.shape[0], n // got.shape[0], n), BF16)],
+        compiler_params=pltpu.CompilerParams(vmem_limit_bytes=66_500_000),
         cost_estimate=pl.CostEstimate(flops=2 * n**3 * 2, bytes_accessed=7 << 20, transcendentals=0),
         name="state",
     )(got, factor, moment, left, right)
@@ -255,12 +285,12 @@
     low = energy - high - middle
     row = lax.broadcasted_iota(jnp.int32, energy.shape, 0)
     packed = jnp.where(row == 0, high, jnp.where(row == 1, middle, low)).astype(BF16)
-    packed = jnp.concatenate([packed] * (out_ref.shape[2] // 128), axis=1)
     for chip in range(chips):
         block = source_ref[2 * chip + core]
         mine = lax.rem(block, 2) == core
-        out_ref[chip, :rows, :] = jnp.where(mine, own_ref[block // 2], other_ref[block // 2])
-        out_ref[chip, rows:, :] = packed
+        for part, high, wide in tiles(rows, own_ref.shape[2]):
+            out_ref[chip, part, :] = jnp.where(mine, own_ref[block // 2, high, wide], other_ref[block // 2, high, wide])
+        out_ref[chip, out_ref.shape[1] - 8 :, :] = packed
 
 
 def return_kernel(slots_ref, own_ref, other_ref, out_ref):
@@ -271,11 +301,10 @@
         out_ref[i] = jnp.where(mine, own_ref[slot // 2], other_ref[slot // 2])
 
 
-def pick_call(kernel, rows, scratch, operands):
-    chips, size = operands[1].shape[0], operands[1].shape[2]
+def pick_call(kernel, shape, scratch, operands):
     return pl.pallas_call(
         kernel,
-        out_shape=jax.ShapeDtypeStruct((chips, rows, size), BF16),
+        out_shape=jax.ShapeDtypeStruct(shape, BF16),
         in_specs=[pl.BlockSpec(memory_space=pltpu.SMEM)]
         + [pl.BlockSpec(memory_space=pltpu.VMEM)] * (len(operands) - 1),
         out_specs=pl.BlockSpec(memory_space=pltpu.VMEM),
@@ -309,23 +338,26 @@
         )
         for s in range(1, tensor_count)
     ]
-    turned, *halves = moment_call(left_basis, right_basis, moment)
-    moved, turned = lax.optimization_barrier((moved, turned))
     for part in moved:
         energy = energy + part
     energy = energy + lax.ppermute(energy, "shard", swap)
     other = lax.ppermute(arrived, "shard", swap)
     routed = pick_call(
-        route_kernel, rows + 8, [pltpu.SMEM((shard_count,), jnp.int32)], (assignment, arrived, other, energy)
+        route_kernel,
+        (chips, rows * size // 128 + 8, 128),
+        [pltpu.SMEM((shard_count,), jnp.int32)],
+        (assignment, arrived, other, energy),
     )
     got = exchange(routed)
-    left_basis_new = basis_call(left_stats, left_basis)
+    turned, *halves = moment_call(left_basis, right_basis, moment)
+    left_half = open_basis(left_stats, left_basis, 1)
     update, second_new, factor = step_call(entries, got, halves, turned, second)
     returned = exchange(update)
-    right_basis_new = basis_call(right_stats, right_basis)
+    right_basis_new = open_basis(right_stats, right_basis, NS_ITERS)
     other = lax.ppermute(returned, "shard", swap)
-    picked = pick_call(return_kernel, rows, [], (assignment, returned, other))
+    picked = pick_call(return_kernel, (chips, rows, size), [], (assignment, returned, other))
     update_out = exchange(picked).reshape(size, size)
+    left_basis_new = close_basis(left_half, NS_ITERS - 1)
     moment_new, left_new, right_new = state_call(got, factor, moment, left_stats, right_stats)
 
     states = (moment_new, second_new, left_new, right_new, left_basis_new, right_basis_new)

time: 102 us -> 104 us (1.020); the launches traced: 102 us -> 102 us
  blocking collectives: 50.6 us -> 33.3 us
  Pallas kernels: 32.5 us -> 41.1 us
  waiting for transfers between devices: 3.38 us -> 11.4 us
  starting transfers between devices: 11.1 us -> 14.6 us
  local copies, waits for them, and re-layouts: 3.13 us -> 0.8 us
    all_to_all x3 -> x2, blocking collectives: 50.6 us -> 33.3 us  [exchange(): return lax.all_to_all(pieces, 'shard', 0, 0, axis_index_groups=same_core)]
    pallas_call x4 -> x5, Pallas kernels: 17.6 us -> 24.2 us  [the longest x3 21.1 us: basis_call(): pl.pallas_call(functools.partial(kernel, sweeps), out_shape=jax.ShapeDtyp...]
    all_to_all x1 -> x2, waiting for transfers between devices: 2.21 us -> 7.61 us  [exchange(): return lax.all_to_all(pieces, 'shard', 0, 0, axis_index_groups=same_core)]
    all_to_all x1 -> x2, starting transfers between devices: 4.47 us -> 8.04 us  [exchange(): return lax.all_to_all(pieces, 'shard', 0, 0, axis_index_groups=same_core)]
    ppermute x3, waiting for transfers between devices: 0.01 us -> 2.6 us  [shards(): lax.ppermute(energy, 'tensor', [(i, (i + s) % tensor_count) for i in rang...]
    unnamed x19 -> x5, local copies, waits for them, and re-layouts: 3.13 us -> 0.8 us
    pallas_call x1, Pallas kernels: 2.27 us -> 4.35 us  [state_call(): pl.pallas_call(state_kernel, out_shape=(full,) * 3, in_specs=[pl.BlockSpe...]
  transfers between devices with their start and end apart: 7 -> 8, of which waited for: 2 -> 4; matrix products, arithmetic and copies ran while one was open for 0% -> 0% of each run, Pallas kernels for 23% -> 30%
where the time goes in v1:
time: 104 us; the launch traced here: 102 us
  Pallas kernels  41.1 us (40%)
  blocking collectives  33.3 us (32%)
  starting transfers between devices  14.6 us (14%)
  waiting for transfers between devices  11.4 us (11%)
    all_to_all x2, blocking collectives, exchange(): return lax.all_to_all(pieces, 'shard', 0, 0, axis_index_groups=same_core)  33.3 us
    pallas_call x3, Pallas kernels, basis_call(): pl.pallas_call(functools.partial(kernel, sweeps), out_shape=jax.ShapeDtyp...  21.1 us
    all_to_all x2, starting transfers between devices, exchange(): return lax.all_to_all(pieces, 'shard', 0, 0, axis_index_groups=same_core)  8.04 us
    all_to_all x2, waiting for transfers between devices, exchange(): return lax.all_to_all(pieces, 'shard', 0, 0, axis_index_groups=same_core)  7.61 us
    pallas_call x1, Pallas kernels, step_call(): pl.pallas_call(functools.partial(step_kernel, entries), out_shape=(jax.Sh...  7.32 us
    ppermute x3, starting transfers between devices, shards(): lax.ppermute(energy, 'tensor', [(i, (i + s) % tensor_count) for i in rang...  6.58 us
    pallas_call x1, Pallas kernels, moment_call(): pl.pallas_call(moment_kernel, out_shape=(jax.ShapeDtypeStruct((n, n), F32...  4.9 us
    pallas_call x1, Pallas kernels, state_call(): pl.pallas_call(state_kernel, out_shape=(full,) * 3, in_specs=[pl.BlockSpe...  4.35 us
  transfers between devices with their start and end apart: 8, of which 4 were waited for; matrix products, arithmetic and copies ran while one was open for 0% of the time, Pallas kernels for 30%

profile of v1, /device:TPU:0, one launch (start us, length us, event | category | flops | bytes accessed | tf_op | source)
XLA Modules:
  0.0 102.0 jit_solution(13314319598626949455)
XLA Ops:
  0.6 0.0 copy-start
  0.6 18.8 %all_to_all.20.own_ref = bf16[16,32,512]{2,1,0:T(8,128)(2,1)S(1)} all-to-all(bf16[16,32,512]{2,1,0:T(8,128)(2,1)} %bitcast.14), channel_id=1, replica_groups={{0,8,16,24,32,40,48,56,64,72,80,88,96,104,112,120},{4,12,20,28,36,44,52..., dimensions={0} | all-to-all | bytes 1048576 | tf_op jit(solution)/shard_map/all_to_all | solution.py:331
  19.5 0.0 collective-permute-start
  19.5 0.0 copy-done
  19.5 0.4 energy.1
  19.9 2.0 %collective-permute-start.1 = (f32[8,128]{1,0:T(8,128)S(1)}, f32[8,128]{1,0:T(8,128)S(1)}, u32[]{:S(2)}, u32[]{:S(2)}) collective-permute-start(f32[8,128]{1,0:T(8,128)S(1)} %energy.1), channel_id=1, source_target_pairs={{0,1},{1,2},{2,3},{3,0},{4,5},{5,6},{6,7},{7,4},{8,9},{9,10},{10,1... | collective-permute-start | bytes 12296 | tf_op jit(solution)/shard_map/ppermute | solution.py:336
  21.9 3.6 %collective-permute-start.2 = (f32[8,128]{1,0:T(8,128)S(1)}, f32[8,128]{1,0:T(8,128)S(1)}, u32[]{:S(2)}, u32[]{:S(2)}) collective-permute-start(f32[8,128]{1,0:T(8,128)S(1)} %energy.1), channel_id=1, source_target_pairs={{0,2},{1,3},{2,0},{3,1},{4,6},{5,7},{6,4},{7,5},{8,10},{9,11},{10,... | collective-permute-start | bytes 12296 | tf_op jit(solution)/shard_map/ppermute | solution.py:336
  25.4 1.0 collective-permute-start.3
  26.4 0.0 collective-permute-done.1
  26.4 0.6 collective-permute-done.2
  27.1 2.0 %collective-permute-done.3 = f32[8,128]{1,0:T(8,128)S(1)} collective-permute-done((f32[8,128]{1,0:T(8,128)S(1)}, f32[8,128]{1,0:T(8,128)S(1)}, u32[]{:S(2)}, u32[]{:S(2)}) %collective-permute-start.3) | collective-permute-done | bytes 4128 | tf_op jit(solution)/shard_map/ppermute | solution.py:336
  29.0 0.0 copy-start.1
  29.1 0.0 collective-permute-start.4
  29.1 1.2 %collective-permute-done.4 = f32[8,128]{1,0:T(8,128)S(1)} collective-permute-done((f32[8,128]{1,0:T(8,128)S(1)}, f32[8,128]{1,0:T(8,128)S(1)}, u32[]{:S(2)}, u32[]{:S(2)}) %collective-permute-start.4) | collective-permute-done | bytes 4128 | tf_op jit(solution)/shard_map/ppermute | solution.py:343
  30.2 0.0 collective-permute-done.other_ref
  30.2 0.0 copy-done.1
  30.2 1.6 %shard_map.135 = bf16[16,136,128]{2,1,0:T(8,128)(2,1)} custom-call(s32[1,32]{1,0:T(1,128)S(1)} %copy-done.1, bf16[16,32,512]{2,1,0:T(8,128)(2,1)S(1)} %all_to_all.20.own_ref, bf16[16,32,512]{2,1,0:T(8,128)(2,1)S(1)} %collective-permute-done.other_ref, f32[8,128]{1,0:T(8,128)S(1)} %add.15.energy_ref), custom_call_target="tpu_custom_call" | custom-call | bytes 2097152 | tf_op jit(solution)/shard_map/pallas_call | solution.py:305
  31.8 4.2 %all-to-all-start.1 = ((bf16[16,136,128]{2,1,0:T(8,128)(2,1)}), bf16[16,136,128]{2,1,0:T(8,128)(2,1)}, u32[]{:S(2)}, u32[]{:S(2)}) async-start(bf16[16,136,128]{2,1,0:T(8,128)(2,1)} %shard_map.135), calls=%async_computation.1 | async-start | bytes 1114112 | tf_op jit(solution)/shard_map/all_to_all | solution.py:331
  36.1 4.9 %turn.1 = (f32[512,512]{1,0:T(8,128)}, bf16[512,512]{1,0:T(8,128)(2,1)}, bf16[512,512]{1,0:T(8,128)(2,1)}, bf16[512,512]{1,0:T(8,128)(2,1)}, bf16[512,512]{1,0:T...) custom-call(f32[512,512]{1,0:T(8,128)} %bitcast.23, f32[512,512]{1,0:T(8,128)} %bitcast.25, ...), custom_call_target="tpu_custom_call" | custom-call | flops 1610612736 | bytes 7340032 | tf_op jit(solution)/shard_map/turn/pallas_call | solution.py:120
  41.0 7.6 %all-to-all-done.1.got_hbm.got_ref = bf16[16,136,128]{2,1,0:T(8,128)(2,1)} async-done(((bf16[16,136,128]{2,1,0:T(8,128)(2,1)}), bf16[16,136,128]{2,1,0:T(8,128)(2,1)}, u32[]{:S(2)}, u32[]{:S(2)}) %all-to-all-start.1) | async-done | bytes 557088 | tf_op jit(solution)/shard_map/all_to_all | solution.py:331
  48.6 7.3 %step.1 = (bf16[16,32,512]{2,1,0:T(8,128)(2,1)}, f32[512,512]{1,0:T(8,128)}, f32[8,128]{1,0:T(8,128)}) custom-call(bf16[16,136,128]{2,1,0:T(8,128)(2,1)} %all-to-all-done.1.got_hbm.got_ref, bf16[512,512]{1,0:T(8,128)(2,1)} %get-tuple-element.20.lth_hbm, bf16[512,512]{1,0:T(8,128)(2,1)} %get-tuple-element.21.ltl_hbm, ...), custom_call_target="tpu_custom_call" | custom-call | flops 2952790016 | bytes 7340032 | tf_op jit(solution)/shard_map/step/pallas_call | solution.py:209
  55.9 14.5 %all_to_all.21.own_ref = bf16[16,32,512]{2,1,0:T(8,128)(2,1)S(1)} all-to-all(bf16[16,32,512]{2,1,0:T(8,128)(2,1)} %get-tuple-element.27), channel_id=1, replica_groups={{0,8,16,24,32,40,48,56,64,72,80,88,96,104,112,120},{4,12,20,28,36,44,52..., dimensions={0} | all-to-all | bytes 1048576 | tf_op jit(solution)/shard_map/all_to_all | solution.py:331
  70.5 0.0 collective-permute-start.5
  70.5 6.7 %shard_map.137.start_ref = f32[512,512]{1,0:T(8,128)} custom-call(f32[512,512]{1,0:T(8,128)} %bitcast.18, f32[512,512]{1,0:T(8,128)} %bitcast.24), custom_call_target="tpu_custom_call" | custom-call | flops 2415919104 | bytes 3145728 | tf_op jit(solution)/shard_map/pallas_call | solution.py:87
  77.2 5.1 %shard_map.138 = f32[512,512]{1,0:T(8,128)} custom-call(f32[512,512]{1,0:T(8,128)} %shard_map.137.start_ref), custom_call_target="tpu_custom_call" | custom-call | flops 2415919104 | bytes 3145728 | tf_op jit(solution)/shard_map/pallas_call | solution.py:87
  82.3 0.0 collective-permute-done.5.other_ref
  82.3 1.5 %shard_map.136 = bf16[16,32,512]{2,1,0:T(8,128)(2,1)} custom-call(s32[1,32]{1,0:T(1,128)S(1)} %copy-done.1, bf16[16,32,512]{2,1,0:T(8,128)(2,1)S(1)} %all_to_all.21.own_ref, bf16[16,32,512]{2,1,0:T(8,128)(2,1)S(1)} %collective-permute-done.5.other_ref), custom_call_target="tpu_custom_call" | custom-call | bytes 2097152 | tf_op jit(solution)/shard_map/pallas_call | solution.py:305
  83.8 3.8 %all-to-all-start.3 = ((bf16[16,32,512]{2,1,0:T(8,128)(2,1)}), bf16[16,32,512]{2,1,0:T(8,128)(2,1)S(1)}, u32[]{:S(2)}, u32[]{:S(2)}) async-start(bf16[16,32,512]{2,1,0:T(8,128)(2,1)} %shard_map.136), calls=%async_computation.3 | async-start | bytes 1048576 | tf_op jit(solution)/shard_map/all_to_all | solution.py:331
  87.6 9.3 %shard_map.139 = f32[512,512]{1,0:T(8,128)} custom-call(f32[512,512]{1,0:T(8,128)} %bitcast.20, f32[512,512]{1,0:T(8,128)} %bitcast.26), custom_call_target="tpu_custom_call" | custom-call | flops 4831838208 | bytes 3145728 | tf_op jit(solution)/shard_map/pallas_call | solution.py:87
  96.8 4.3 %state.1 = (f32[512,512]{1,0:T(8,128)}, f32[512,512]{1,0:T(8,128)}, f32[512,512]{1,0:T(8,128)}) custom-call(bf16[16,136,128]{2,1,0:T(8,128)(2,1)} %all-to-all-done.1.got_hbm.got_ref, f32[8,128]{1,0:T(8,128)} %get-tuple-element.28.factor_ref, f32[512,512]{1,0:T(8,128)} %bitcast.17, f32[512,512]{1,0:T(8,128)} %bitcast.19, f32[512,512]{1,0:T(8,128)} %bitcast.21), custom_call_target="tpu_custom_call" | custom-call | flops 536870912 | bytes 7340032 | tf_op jit(solution)/shard_map/state/pallas_call | solution.py:248
  101.2 0.0 all-to-all-done.3
  101.2 0.8 copy.16
  (2 shorter events, 0.0 us)
Async XLA Ops:
  0.6 18.8 %copy-start = (bf16[512,512]{1,0:T(8,128)(2,1)S(1)}, bf16[512,512]{1,0:T(8,128)(2,1)}, u32[]{:S(2)}) copy-start(bf16[512,512]{1,0:T(8,128)(2,1)} %grads_ref.1) | copy-start | bytes 1572868
  19.5 10.8 %collective-permute-start = (bf16[16,32,512]{2,1,0:T(8,128)(2,1)S(1)}, bf16[16,32,512]{2,1,0:T(8,128)(2,1)S(1)}, u32[]{:S(2)}, u32[]{:S(2)}) collective-permute-start(bf16[16,32,512]{2,1,0:T(8,128)(2,1)S(1)} %all_to_all.20.own_ref), channel_id=1, source_target_pairs={{0,4},{4,0},{8,12},{12,8},{16,20},{20,16},{24,28},{28,24},{32,36},... | collective-permute-start | bytes 1572872 | tf_op jit(solution)/shard_map/ppermute | solution.py:344
  19.9 6.6 %collective-permute-start.1 = (f32[8,128]{1,0:T(8,128)S(1)}, f32[8,128]{1,0:T(8,128)S(1)}, u32[]{:S(2)}, u32[]{:S(2)}) collective-permute-start(f32[8,128]{1,0:T(8,128)S(1)} %energy.1), channel_id=1, source_target_pairs={{0,1},{1,2},{2,3},{3,0},{4,5},{5,6},{6,7},{7,4},{8,9},{9,10},{10,1... | collective-permute-start | bytes 12296 | tf_op jit(solution)/shard_map/ppermute | solution.py:336
  21.9 5.2 %collective-permute-start.2 = (f32[8,128]{1,0:T(8,128)S(1)}, f32[8,128]{1,0:T(8,128)S(1)}, u32[]{:S(2)}, u32[]{:S(2)}) collective-permute-start(f32[8,128]{1,0:T(8,128)S(1)} %energy.1), channel_id=1, source_target_pairs={{0,2},{1,3},{2,0},{3,1},{4,6},{5,7},{6,4},{7,5},{8,10},{9,11},{10,... | collective-permute-start | bytes 12296 | tf_op jit(solution)/shard_map/ppermute | solution.py:336
  25.4 3.6 %collective-permute-start.3 = (f32[8,128]{1,0:T(8,128)S(1)}, f32[8,128]{1,0:T(8,128)S(1)}, u32[]{:S(2)}, u32[]{:S(2)}) collective-permute-start(f32[8,128]{1,0:T(8,128)S(1)} %energy.1), channel_id=1, source_target_pairs={{0,3},{1,0},{2,1},{3,2},{4,7},{5,4},{6,5},{7,6},{8,11},{9,8},{10,9... | collective-permute-start | bytes 12296 | tf_op jit(solution)/shard_map/ppermute | solution.py:336
  29.0 1.2 %copy-start.1 = (s32[1,32]{1,0:T(1,128)S(1)}, s32[1,32]{1,0:T(1,128)}, u32[]{:S(2)}) copy-start(s32[1,32]{1,0:T(1,128)} %slots_ref.3) | copy-start | bytes 388
  29.1 1.2 %collective-permute-start.4 = (f32[8,128]{1,0:T(8,128)S(1)}, f32[8,128]{1,0:T(8,128)S(1)}, u32[]{:S(2)}, u32[]{:S(2)}) collective-permute-start(f32[8,128]{1,0:T(8,128)S(1)} %add_add_fusion), channel_id=1, source_target_pairs={{0,4},{4,0},{8,12},{12,8},{16,20},{20,16},{24,28},{28,24},{32,36},... | collective-permute-start | bytes 12296 | tf_op jit(solution)/shard_map/ppermute | solution.py:343
  31.8 16.8 %all-to-all-start.1 = ((bf16[16,136,128]{2,1,0:T(8,128)(2,1)}), bf16[16,136,128]{2,1,0:T(8,128)(2,1)}, u32[]{:S(2)}, u32[]{:S(2)}) async-start(bf16[16,136,128]{2,1,0:T(8,128)(2,1)} %shard_map.135), calls=%async_computation.1 | async-start | bytes 1114112 | tf_op jit(solution)/shard_map/all_to_all | solution.py:331
  70.5 11.9 %collective-permute-start.5 = (bf16[16,32,512]{2,1,0:T(8,128)(2,1)S(1)}, bf16[16,32,512]{2,1,0:T(8,128)(2,1)S(1)}, u32[]{:S(2)}, u32[]{:S(2)}) collective-permute-start(bf16[16,32,512]{2,1,0:T(8,128)(2,1)S(1)} %all_to_all.21.own_ref), channel_id=1, source_target_pairs={{0,4},{4,0},{8,12},{12,8},{16,20},{20,16},{24,28},{28,24},{32,36},... | collective-permute-start | bytes 1572872 | tf_op jit(solution)/shard_map/ppermute | solution.py:357
  83.8 17.4 %all-to-all-start.3 = ((bf16[16,32,512]{2,1,0:T(8,128)(2,1)}), bf16[16,32,512]{2,1,0:T(8,128)(2,1)S(1)}, u32[]{:S(2)}, u32[]{:S(2)}) async-start(bf16[16,32,512]{2,1,0:T(8,128)(2,1)} %shard_map.136), calls=%async_computation.3 | async-start | bytes 1048576 | tf_op jit(solution)/shard_map/all_to_all | solution.py:331

commit v2 on v1

--- a/solution.py
+++ b/solution.py
@@ -47,7 +47,7 @@
     return mxu(a_high, bh[...], dims) + (mxu(a_high, bl[...], dims) + mxu(al[at, :], bh[...], dims))
 
 
-def sweep(y, ah, al, xh, xl, gh, gl):
+def polynomial(y, ah, al, xh, xl, gh, gl):
     store_split(y[...], xh, xl)
     for at in blocks(y):
         store_split(prod3(xh, xl, xh, xl, at, NT), gh, gl, at)
@@ -55,78 +55,182 @@
         square = prod3(gh, gl, gh, gl, at)
         gram = gh[at, :].astype(F32) + gl[at, :].astype(F32)
         store_split(QUINTIC_B * gram + QUINTIC_C * square, ah, al, at)
+
+
+def sweep(y, ah, al, xh, xl, gh, gl):
+    polynomial(y, ah, al, xh, xl, gh, gl)
     for at in blocks(y):
         y[at, :] = QUINTIC_A * y[at, :] + prod3(ah, al, xh, xl, at)
 
 
-def open_kernel(sweeps, stats_ref, basis_ref, y, ah, al, xh, xl, gh, gl):
-    store_split(stats_ref[...], ah, al)
-    store_split(basis_ref[...], xh, xl)
+def last_sweep(y, ah, al, xh, xl, gh, gl, out, out_hbm, stores):
+    polynomial(y, ah, al, xh, xl, gh, gl)
+    gh[...] = xh[...].T
+    gl[...] = xl[...].T
+    before = None
+    for at in blocks(y):
+        rows = gh[at, :].astype(F32) + gl[at, :].astype(F32)
+        out[at, :] = QUINTIC_A * rows + prod3(gh, gl, ah, al, at)
+        if before is not None:
+            stores.add(out.at[before, :], out_hbm.at[before, :])
+        before = at
+    stores.add(out.at[before, :], out_hbm.at[before, :])
+
+
+def make_loads(pairs, sems):
+    return [pltpu.make_async_copy(source, target, sems.at[i]) for i, (source, target) in enumerate(pairs)]
+
+
+class Stores:
+    def __init__(self, sems):
+        self.sems, self.copies = sems, []
+
+    def add(self, source, target):
+        copy = pltpu.make_async_copy(source, target, self.sems.at[len(self.copies)])
+        copy.start()
+        self.copies.append(copy)
+
+    def wait(self):
+        for copy in self.copies:
+            copy.wait()
+
+
+def first_iterate(y, ah, al, bth, btl):
     total = jnp.zeros((), F32)
-    for at in blocks(stats_ref):
-        part = prod3(ah, al, xh, xl, at)
+    for at in blocks(y):
+        part = prod3(bth, btl, ah, al, at, NT)
         y[at, :] = part
         total = total + jnp.sum(part * part)
-    scale = lax.rsqrt(total + 1e-12)
-    y[...] = (y[...] * scale).T
-    for _ in range(sweeps):
+    y[...] = y[...] * lax.rsqrt(total + 1e-12)
+
+
+def early_kernel(left_hbm, stats_hbm, right_hbm, moment_hbm,
+                 y_hbm, pmq_hbm, lth_hbm, ltl_hbm, lh_hbm, ll_hbm, rh_hbm, rl_hbm,
+                 left, stats, right, moment, y, pmq, lth, ltl, lh, ll, rh, rl, ah, al, xh, xl, gh, gl,
+                 in_sems, out_sems):
+    pairs = ((left_hbm, left), (stats_hbm, stats), (right_hbm, right), (moment_hbm, moment))
+    loads = make_loads(pairs, in_sems)
+    stores = Stores(out_sems)
+    loads[0].start()
+    loads[1].start()
+    loads[0].wait()
+    store_split(left[...].T, lth, ltl)
+    loads[1].wait()
+    loads[2].start()
+    loads[3].start()
+    store_split(stats[...], ah, al)
+    first_iterate(y, ah, al, lth, ltl)
+    store_split(left[...], lh, ll)
+    for source, target in ((lth, lth_hbm), (ltl, ltl_hbm), (lh, lh_hbm), (ll, ll_hbm)):
+        stores.add(source, target)
+    sweep(y, ah, al, xh, xl, gh, gl)
+    loads[2].wait()
+    store_split(right[...], rh, rl)
+    stores.add(y, y_hbm)
+    loads[3].wait()
+    store_split(moment[...], xh, xl)
+    stores.add(rh, rh_hbm)
+    stores.add(rl, rl_hbm)
+    before = None
+    for at in blocks(pmq):
+        high, low = split(prod3(lth, ltl, xh, xl, at))
+        if before is not None:
+            stores.add(pmq.at[before, :], pmq_hbm.at[before, :])
+        pmq[at, :] = mxu(high, rh[...]) + (mxu(high, rl[...]) + mxu(low, rh[...]))
+        before = at
+    stores.add(pmq.at[before, :], pmq_hbm.at[before, :])
+    stores.wait()
+
+
+def right_kernel(stats_hbm, basis_hbm, out_hbm, stats, basis, y, ah, al, xh, xl, gh, gl, in_sems, out_sems):
+    loads = make_loads(((basis_hbm, basis), (stats_hbm, stats)), in_sems)
+    stores = Stores(out_sems)
+    for load in loads:
+        load.start()
+    loads[0].wait()
+    store_split(basis[...].T, xh, xl)
+    loads[1].wait()
+    store_split(stats[...], ah, al)
+    first_iterate(y, ah, al, xh, xl)
+    for _ in range(NS_ITERS - 1):
         sweep(y, ah, al, xh, xl, gh, gl)
-    if sweeps == NS_ITERS:
-        y[...] = y[...].T
-
-
-def close_kernel(sweeps, start_ref, out_ref, y, ah, al, xh, xl, gh, gl):
-    y[...] = start_ref[...]
-    for _ in range(sweeps):
-        sweep(y, ah, al, xh, xl, gh, gl)
-    out_ref[...] = y[...].T
-
-
-def basis_call(kernel, sweeps, operands, extra):
-    n = operands[0].shape[0]
+    last_sweep(y, ah, al, xh, xl, gh, gl, stats, out_hbm, stores)
+    stores.wait()
+
+
+def late_kernel(y_hbm, got_hbm, factor_hbm, moment_hbm, left_hbm, right_hbm,
+                basis_hbm, moment_out, left_out, right_out,
+                y, got, factor_ref, moment, left, right, tile_ref, turned, out, ah, al, xh, xl, gh, gl,
+                in_sems, out_sems):
+    n, rows = moment.shape[0], tile_ref.shape[1]
+    pairs = ((y_hbm, y), (got_hbm, got), (factor_hbm, factor_ref))
+    pairs += ((moment_hbm, moment), (left_hbm, left), (right_hbm, right))
+    loads = make_loads(pairs, in_sems)
+    stores = Stores(out_sems)
+    loads[0].start()
+    loads[0].wait()
+    for load in loads[1:]:
+        load.start()
+    last_sweep(y, ah, al, xh, xl, gh, gl, out, basis_hbm, stores)
+    for load in loads[1:]:
+        load.wait()
+    for part, high, wide in tiles(rows, n):
+        tile_ref[:, high, wide] = got[:, part, :]
+    tile = tile_ref[...].reshape(n, n)
+    turned[...] = tile.T
+    factor = factor_ref[0:1, 0:1]
+    scale = (1.0 - BETA_STATS) * factor * factor / n
+    before = None
+    for at in blocks(moment):
+        mine = tile[at.start : at.start + BLK, :]
+        moment[at, :] = BETA_MOMENT * moment[at, :] + (1.0 - BETA_MOMENT) * (factor * mine.astype(F32))
+        left[at, :] = BETA_STATS * left[at, :] + scale * mxu(mine, tile, NT)
+        right[at, :] = BETA_STATS * right[at, :] + scale * mxu(turned[at, :], tile)
+        for part in (before, at if at.start + BLK == n else None):
+            if part is not None:
+                for source, target in ((moment, moment_out), (left, left_out), (right, right_out)):
+                    stores.add(source.at[part, :], target.at[part, :])
+        before = at
+    stores.wait()
+
+
+def window_call(kernel, operands, outs, scratch, passes, limit):
+    hbm = pl.BlockSpec(memory_space=pltpu.HBM)
+    n = outs[0].shape[0]
     return pl.pallas_call(
-        functools.partial(kernel, sweeps),
-        out_shape=jax.ShapeDtypeStruct((n, n), F32),
-        in_specs=[pl.BlockSpec(memory_space=pltpu.VMEM)] * len(operands),
-        out_specs=pl.BlockSpec(memory_space=pltpu.VMEM),
-        scratch_shapes=[pltpu.VMEM((n, n), F32)] * extra + [pltpu.VMEM((n, n), BF16)] * 6,
-        compiler_params=pltpu.CompilerParams(vmem_limit_bytes=64_900_000),
-        cost_estimate=pl.CostEstimate(flops=2 * n**3 * 9 * sweeps, bytes_accessed=3 << 20, transcendentals=0),
+        kernel,
+        out_shape=outs,
+        in_specs=[hbm] * len(operands),
+        out_specs=[hbm] * len(outs),
+        scratch_shapes=scratch + [pltpu.SemaphoreType.DMA((8,)), pltpu.SemaphoreType.DMA((12,))],
+        compiler_params=pltpu.CompilerParams(vmem_limit_bytes=limit),
+        cost_estimate=pl.CostEstimate(flops=2 * n**3 * passes, bytes_accessed=8 << 20, transcendentals=0),
     )(*operands)
 
 
-def open_basis(stats, basis, sweeps):
-    return basis_call(open_kernel, sweeps, (stats, basis), 0)
-
-
-def close_basis(start, sweeps):
-    return basis_call(close_kernel, sweeps, (start,), 1)
-
-
-def moment_kernel(left_ref, right_ref, moment_ref, out_ref, lth, ltl, lh, ll, rh, rl, mh, ml):
-    left = left_ref[...]
-    store_split(left, lh, ll)
-    store_split(left.T, lth, ltl)
-    store_split(right_ref[...], rh, rl)
-    store_split(moment_ref[...], mh, ml)
-    for at in blocks(left_ref):
-        high, low = split(prod3(lth, ltl, mh, ml, at))
-        out_ref[at, :] = mxu(high, rh[...]) + (mxu(high, rl[...]) + mxu(low, rh[...]))
-
-
-def moment_call(left, right, moment):
+def early_call(left, stats, right, moment):
     n = left.shape[0]
-    half = jax.ShapeDtypeStruct((n, n), BF16)
-    return pl.pallas_call(
-        moment_kernel,
-        out_shape=(jax.ShapeDtypeStruct((n, n), F32),) + (half,) * 6,
-        in_specs=[pl.BlockSpec(memory_space=pltpu.VMEM)] * 3,
-        out_specs=[pl.BlockSpec(memory_space=pltpu.VMEM)] * 7,
-        scratch_shapes=[pltpu.VMEM((n, n), BF16)] * 2,
-        compiler_params=pltpu.CompilerParams(vmem_limit_bytes=65_600_000),
-        cost_estimate=pl.CostEstimate(flops=2 * n**3 * 6, bytes_accessed=7 << 20, transcendentals=0),
-        name="turn",
-    )(left, right, moment)
+    full, half = (n, n), pltpu.VMEM((n, n), BF16)
+    outs = (jax.ShapeDtypeStruct(full, F32),) * 2 + (jax.ShapeDtypeStruct(full, BF16),) * 6
+    scratch = [pltpu.VMEM(full, F32)] * 6 + [half] * 12
+    return window_call(early_kernel, (left, stats, right, moment), outs, scratch, 18, 65_600_000)
+
+
+def right_call(stats, basis):
+    n = stats.shape[0]
+    scratch = [pltpu.VMEM((n, n), F32)] * 3 + [pltpu.VMEM((n, n), BF16)] * 6
+    outs = (jax.ShapeDtypeStruct((n, n), F32),)
+    return window_call(right_kernel, (stats, basis), outs, scratch, 21, 65_600_000)[0]
+
+
+def late_call(half, got, factor, moment, left, right):
+    n = half.shape[0]
+    full = pltpu.VMEM((n, n), F32)
+    scratch = [full, pltpu.VMEM(got.shape, BF16), pltpu.VMEM(factor.shape, F32)] + [full] * 3
+    scratch += [pltpu.VMEM((got.shape[0], n // got.shape[0], n), BF16), pltpu.VMEM((n, n), BF16), full]
+    scratch += [pltpu.VMEM((n, n), BF16)] * 6
+    outs = (jax.ShapeDtypeStruct((n, n), F32),) * 4
+    return window_call(late_kernel, (half, got, factor, moment, left, right), outs, scratch, 11, 65_600_000)
 
 
 def tiles(rows, n):
@@ -226,37 +330,6 @@
     )(got, lth, ltl, rh, rl, second, pmq, lh, ll)
 
 
-def state_kernel(got_ref, factor_ref, moment_ref, left_ref, right_ref, moment_out, left_out, right_out, tile_ref):
-    n = moment_ref.shape[0]
-    rows = tile_ref.shape[1]
-    for part, high, wide in tiles(rows, n):
-        tile_ref[:, high, wide] = got_ref[:, part, :]
-    tile = tile_ref[...].reshape(n, n)
-    factor = factor_ref[0:1, 0:1]
-    scale = (1.0 - BETA_STATS) * factor * factor / n
-    turned = tile.T
-    for at in blocks(moment_ref):
-        mine = tile[at.start : at.start + BLK, :]
-        moment_out[at, :] = BETA_MOMENT * moment_ref[at, :] + (1.0 - BETA_MOMENT) * (factor * mine.astype(F32))
-        left_out[at, :] = BETA_STATS * left_ref[at, :] + scale * mxu(mine, tile, NT)
-        right_out[at, :] = BETA_STATS * right_ref[at, :] + scale * mxu(turned[at.start : at.start + BLK, :], tile)
-
-
-def state_call(got, factor, moment, left, right):
-    n = moment.shape[0]
-    full = jax.ShapeDtypeStruct((n, n), F32)
-    return pl.pallas_call(
-        state_kernel,
-        out_shape=(full,) * 3,
-        in_specs=[pl.BlockSpec(memory_space=pltpu.VMEM)] * 5,
-        out_specs=[pl.BlockSpec(memory_space=pltpu.VMEM)] * 3,
-        scratch_shapes=[pltpu.VMEM((got.shape[0], n // got.shape[0], n), BF16)],
-        compiler_params=pltpu.CompilerParams(vmem_limit_bytes=66_500_000),
-        cost_estimate=pl.CostEstimate(flops=2 * n**3 * 2, bytes_accessed=7 << 20, transcendentals=0),
-        name="state",
-    )(got, factor, moment, left, right)
-
-
 def energy_kernel(grads_ref, out_ref):
     x = grads_ref[...].astype(F32)
     out_ref[...] = jnp.full(out_ref.shape, jnp.sum(x * x))
@@ -349,16 +422,14 @@
         (assignment, arrived, other, energy),
     )
     got = exchange(routed)
-    turned, *halves = moment_call(left_basis, right_basis, moment)
-    left_half = open_basis(left_stats, left_basis, 1)
+    left_half, turned, *halves = early_call(left_basis, left_stats, right_basis, moment)
     update, second_new, factor = step_call(entries, got, halves, turned, second)
     returned = exchange(update)
-    right_basis_new = open_basis(right_stats, right_basis, NS_ITERS)
+    right_basis_new = right_call(right_stats, right_basis)
     other = lax.ppermute(returned, "shard", swap)
     picked = pick_call(return_kernel, (chips, rows, size), [], (assignment, returned, other))
     update_out = exchange(picked).reshape(size, size)
-    left_basis_new = close_basis(left_half, NS_ITERS - 1)
-    moment_new, left_new, right_new = state_call(got, factor, moment, left_stats, right_stats)
+    left_basis_new, moment_new, left_new, right_new = late_call(left_half, got, factor, moment, left_stats, right_stats)
 
     states = (moment_new, second_new, left_new, right_new, left_basis_new, right_basis_new)
     return (update_out,) + tuple(state[None] for state in states)

time: 104 us -> 96.8 us (0.931)
  Pallas kernels: 41.1 us -> 35.8 us
  waiting for transfers between devices: 11.4 us -> 9.2 us
    pallas_call x5 -> x3, Pallas kernels: 30.4 us -> 25.1 us  [window_call(): pl.pallas_call(kernel, out_shape=outs, in_specs=[hbm] * len(operands), ou...]
    all_to_all x2, waiting for transfers between devices: 7.61 us -> 3.53 us  [exchange(): return lax.all_to_all(pieces, 'shard', 0, 0, axis_index_groups=same_core)]
    ppermute x1, waiting for transfers between devices: 0.01 us -> 1.91 us  [shards(): other = lax.ppermute(returned, 'shard', swap)]
  transfers between devices with their start and end apart: 8 -> 8, of which waited for: 4 -> 5; matrix products, arithmetic and copies ran while one was open for 0% -> 0% of each run, Pallas kernels for 30% -> 27%
where the time goes in v2:
time: 96.8 us; the launch traced here: 95.1 us
  Pallas kernels  35.8 us (37%)
  blocking collectives  34 us (35%)
  starting transfers between devices  14.6 us (15%)
  waiting for transfers between devices  9.2 us (10%)
    all_to_all x2, blocking collectives, exchange(): return lax.all_to_all(pieces, 'shard', 0, 0, axis_index_groups=same_core)  34 us
    pallas_call x3, Pallas kernels, window_call(): pl.pallas_call(kernel, out_shape=outs, in_specs=[hbm] * len(operands), ou...  25.1 us
    all_to_all x2, starting transfers between devices, exchange(): return lax.all_to_all(pieces, 'shard', 0, 0, axis_index_groups=same_core)  7.99 us
    pallas_call x1, Pallas kernels, step_call(): pl.pallas_call(functools.partial(step_kernel, entries), out_shape=(jax.Sh...  7.32 us
    ppermute x3, starting transfers between devices, shards(): lax.ppermute(energy, 'tensor', [(i, (i + s) % tensor_count) for i in rang...  6.58 us
    all_to_all x2, waiting for transfers between devices, exchange(): return lax.all_to_all(pieces, 'shard', 0, 0, axis_index_groups=same_core)  3.53 us
    pallas_call x2, Pallas kernels, pick_call(): pl.pallas_call(kernel, out_shape=jax.ShapeDtypeStruct(shape, BF16), in_sp...  3.06 us
    ppermute x3, waiting for transfers between devices, shards(): lax.ppermute(energy, 'tensor', [(i, (i + s) % tensor_count) for i in rang...  2.6 us
  transfers between devices with their start and end apart: 8, of which 5 were waited for; matrix products, arithmetic and copies ran while one was open for 0% of the time, Pallas kernels for 27%

profile of v2, /device:TPU:0, one launch (start us, length us, event | category | flops | bytes accessed | tf_op | source)
XLA Modules:
  0.0 95.1 jit_solution(12278708098310518870)
XLA Ops:
  0.6 0.0 copy-start
  0.6 18.8 %all_to_all.20.own_ref = bf16[16,32,512]{2,1,0:T(8,128)(2,1)S(1)} all-to-all(bf16[16,32,512]{2,1,0:T(8,128)(2,1)} %bitcast.14), channel_id=1, replica_groups={{0,8,16,24,32,40,48,56,64,72,80,88,96,104,112,120},{4,12,20,28,36,44,52..., dimensions={0} | all-to-all | bytes 1048576 | tf_op jit(solution)/shard_map/all_to_all | solution.py:404
  19.5 0.0 collective-permute-start
  19.5 0.0 copy-done
  19.5 0.4 energy.1
  19.9 2.0 %collective-permute-start.1 = (f32[8,128]{1,0:T(8,128)S(1)}, f32[8,128]{1,0:T(8,128)S(1)}, u32[]{:S(2)}, u32[]{:S(2)}) collective-permute-start(f32[8,128]{1,0:T(8,128)S(1)} %energy.1), channel_id=1, source_target_pairs={{0,1},{1,2},{2,3},{3,0},{4,5},{5,6},{6,7},{7,4},{8,9},{9,10},{10,1... | collective-permute-start | bytes 12296 | tf_op jit(solution)/shard_map/ppermute | solution.py:409
  21.9 3.6 %collective-permute-start.2 = (f32[8,128]{1,0:T(8,128)S(1)}, f32[8,128]{1,0:T(8,128)S(1)}, u32[]{:S(2)}, u32[]{:S(2)}) collective-permute-start(f32[8,128]{1,0:T(8,128)S(1)} %energy.1), channel_id=1, source_target_pairs={{0,2},{1,3},{2,0},{3,1},{4,6},{5,7},{6,4},{7,5},{8,10},{9,11},{10,... | collective-permute-start | bytes 12296 | tf_op jit(solution)/shard_map/ppermute | solution.py:409
  25.4 1.0 %collective-permute-start.3 = (f32[8,128]{1,0:T(8,128)S(1)}, f32[8,128]{1,0:T(8,128)S(1)}, u32[]{:S(2)}, u32[]{:S(2)}) collective-permute-start(f32[8,128]{1,0:T(8,128)S(1)} %energy.1), channel_id=1, source_target_pairs={{0,3},{1,0},{2,1},{3,2},{4,7},{5,4},{6,5},{7,6},{8,11},{9,8},{10,9... | collective-permute-start | bytes 12296 | tf_op jit(solution)/shard_map/ppermute | solution.py:409
  26.4 0.0 collective-permute-done.1
  26.4 0.6 collective-permute-done.2
  27.1 2.0 %collective-permute-done.3 = f32[8,128]{1,0:T(8,128)S(1)} collective-permute-done((f32[8,128]{1,0:T(8,128)S(1)}, f32[8,128]{1,0:T(8,128)S(1)}, u32[]{:S(2)}, u32[]{:S(2)}) %collective-permute-start.3) | collective-permute-done | bytes 4128 | tf_op jit(solution)/shard_map/ppermute | solution.py:409
  29.0 0.0 copy-start.1
  29.1 0.0 collective-permute-start.4
  29.1 1.2 %collective-permute-done.4 = f32[8,128]{1,0:T(8,128)S(1)} collective-permute-done((f32[8,128]{1,0:T(8,128)S(1)}, f32[8,128]{1,0:T(8,128)S(1)}, u32[]{:S(2)}, u32[]{:S(2)}) %collective-permute-start.4) | collective-permute-done | bytes 4128 | tf_op jit(solution)/shard_map/ppermute | solution.py:416
  30.2 0.0 collective-permute-done.other_ref
  30.2 0.0 copy-done.1
  30.2 1.6 %shard_map.135 = bf16[16,136,128]{2,1,0:T(8,128)(2,1)} custom-call(s32[1,32]{1,0:T(1,128)S(1)} %copy-done.1, bf16[16,32,512]{2,1,0:T(8,128)(2,1)S(1)} %all_to_all.20.own_ref, bf16[16,32,512]{2,1,0:T(8,128)(2,1)S(1)} %collective-permute-done.other_ref, f32[8,128]{1,0:T(8,128)S(1)} %add.15.energy_ref), custom_call_target="tpu_custom_call" | custom-call | bytes 2097152 | tf_op jit(solution)/shard_map/pallas_call | solution.py:378
  31.8 4.2 %all-to-all-start.1 = ((bf16[16,136,128]{2,1,0:T(8,128)(2,1)}), bf16[16,136,128]{2,1,0:T(8,128)(2,1)}, u32[]{:S(2)}, u32[]{:S(2)}) async-start(bf16[16,136,128]{2,1,0:T(8,128)(2,1)} %shard_map.135), calls=%async_computation.1 | async-start | bytes 1114112 | tf_op jit(solution)/shard_map/all_to_all | solution.py:404
  36.1 9.0 %shard_map.136 = (f32[512,512]{1,0:T(8,128)}, f32[512,512]{1,0:T(8,128)}, bf16[512,512]{1,0:T(8,128)(2,1)}, bf16[512,512]{1,0:T(8,128)(2,1)}, bf16[512,512]{1,0:...) custom-call(f32[512,512]{1,0:T(8,128)} %bitcast.16, ...), custom_call_target="tpu_custom_call" | custom-call | flops 4831838208 | bytes 8388608 | tf_op jit(solution)/shard_map/pallas_call | solution.py:200
  45.1 3.5 %all-to-all-done.1.got_hbm = bf16[16,136,128]{2,1,0:T(8,128)(2,1)} async-done(((bf16[16,136,128]{2,1,0:T(8,128)(2,1)}), bf16[16,136,128]{2,1,0:T(8,128)(2,1)}, u32[]{:S(2)}, u32[]{:S(2)}) %all-to-all-start.1) | async-done | bytes 557088 | tf_op jit(solution)/shard_map/all_to_all | solution.py:404
  48.6 7.3 %step.1 = (bf16[16,32,512]{2,1,0:T(8,128)(2,1)}, f32[512,512]{1,0:T(8,128)}, f32[8,128]{1,0:T(8,128)}) custom-call(bf16[16,136,128]{2,1,0:T(8,128)(2,1)} %all-to-all-done.1.got_hbm, bf16[512,512]{1,0:T(8,128)(2,1)} %get-tuple-element.22.lth_hbm, bf16[512,512]{1,0:T(8,128)(2,1)} %get-tuple-element.23.ltl_hbm, bf16[512,512]{1,0:T(8,128)(2,1)} %get-tuple-element.24.rh_hbm, ...), custom_call_target="tpu_custom_call" | custom-call | flops 2952790016 | bytes 7340032 | tf_op jit(solution)/shard_map/step/pallas_call | solution.py:313
  55.9 15.2 %all_to_all.21.own_ref = bf16[16,32,512]{2,1,0:T(8,128)(2,1)S(1)} all-to-all(bf16[16,32,512]{2,1,0:T(8,128)(2,1)} %get-tuple-element.29), channel_id=1, replica_groups={{0,8,16,24,32,40,48,56,64,72,80,88,96,104,112,120},{4,12,20,28,36,44,52..., dimensions={0} | all-to-all | bytes 1048576 | tf_op jit(solution)/shard_map/all_to_all | solution.py:404
  71.1 0.0 collective-permute-start.5
  71.1 1.9 %collective-permute-done.5.other_ref = bf16[16,32,512]{2,1,0:T(8,128)(2,1)S(1)} collective-permute-done((bf16[16,32,512]{2,1,0:T(8,128)(2,1)S(1)}, bf16[16,32,512]{2,1,0:T(8,128)(2,1)S(1)}, u32[]{:S(2)}, u32[]{:S(2)}) %collective-permute-start.5) | collective-permute-done | bytes 524320 | tf_op jit(solution)/shard_map/ppermute | solution.py:429
  73.0 1.5 %shard_map.137 = bf16[16,32,512]{2,1,0:T(8,128)(2,1)} custom-call(s32[1,32]{1,0:T(1,128)S(1)} %copy-done.1, bf16[16,32,512]{2,1,0:T(8,128)(2,1)S(1)} %all_to_all.21.own_ref, bf16[16,32,512]{2,1,0:T(8,128)(2,1)S(1)} %collective-permute-done.5.other_ref), custom_call_target="tpu_custom_call" | custom-call | bytes 2097152 | tf_op jit(solution)/shard_map/pallas_call | solution.py:378
  74.5 3.8 %all-to-all-start.3 = ((bf16[16,32,512]{2,1,0:T(8,128)(2,1)}), bf16[16,32,512]{2,1,0:T(8,128)(2,1)S(1)}, u32[]{:S(2)}, u32[]{:S(2)}) async-start(bf16[16,32,512]{2,1,0:T(8,128)(2,1)} %shard_map.137), calls=%async_computation.3 | async-start | bytes 1048576 | tf_op jit(solution)/shard_map/all_to_all | solution.py:404
  78.2 9.5 %shard_map.139 = f32[512,512]{1,0:T(8,128)} custom-call(f32[512,512]{1,0:T(8,128)} %bitcast.24, f32[512,512]{1,0:T(8,128)} %bitcast.19), custom_call_target="tpu_custom_call" | custom-call | flops 5637144576 | bytes 8388608 | tf_op jit(solution)/shard_map/pallas_call | solution.py:200
  87.7 6.6 %shard_map.138 = (f32[512,512]{1,0:T(8,128)}, f32[512,512]{1,0:T(8,128)}, f32[512,512]{1,0:T(8,128)}, f32[512,512]{1,0:T(8,128)}) custom-call(f32[512,512]{1,0:T(8,128)} %get-tuple-element.30.y_hbm, bf16[16,136,128]{2,1,0:T(8,128)(2,1)} %all-to-all-done.1.got_hbm, f32[8,128]{1,0:T(8,128)} %get-tuple-element.31.factor_hbm, f32[512,512]{1,0:T(8,128)} %bitcast.23, ...), custom_call_target="tpu_custom_call" | custom-call | flops 2952790016 | bytes 8388608 | tf_op jit(solution)/shard_map/pallas_call | solution.py:200
  94.3 0.0 all-to-all-done.3
  94.3 0.8 copy.16
  (2 shorter events, 0.0 us)
Async XLA Ops:
  0.6 18.8 %copy-start = (bf16[512,512]{1,0:T(8,128)(2,1)S(1)}, bf16[512,512]{1,0:T(8,128)(2,1)}, u32[]{:S(2)}) copy-start(bf16[512,512]{1,0:T(8,128)(2,1)} %grads_ref.1) | copy-start | bytes 1572868
  19.5 10.8 %collective-permute-start = (bf16[16,32,512]{2,1,0:T(8,128)(2,1)S(1)}, bf16[16,32,512]{2,1,0:T(8,128)(2,1)S(1)}, u32[]{:S(2)}, u32[]{:S(2)}) collective-permute-start(bf16[16,32,512]{2,1,0:T(8,128)(2,1)S(1)} %all_to_all.20.own_ref), channel_id=1, source_target_pairs={{0,4},{4,0},{8,12},{12,8},{16,20},{20,16},{24,28},{28,24},{32,36},... | collective-permute-start | bytes 1572872 | tf_op jit(solution)/shard_map/ppermute | solution.py:417
  19.9 6.6 %collective-permute-start.1 = (f32[8,128]{1,0:T(8,128)S(1)}, f32[8,128]{1,0:T(8,128)S(1)}, u32[]{:S(2)}, u32[]{:S(2)}) collective-permute-start(f32[8,128]{1,0:T(8,128)S(1)} %energy.1), channel_id=1, source_target_pairs={{0,1},{1,2},{2,3},{3,0},{4,5},{5,6},{6,7},{7,4},{8,9},{9,10},{10,1... | collective-permute-start | bytes 12296 | tf_op jit(solution)/shard_map/ppermute | solution.py:409
  21.9 5.2 %collective-permute-start.2 = (f32[8,128]{1,0:T(8,128)S(1)}, f32[8,128]{1,0:T(8,128)S(1)}, u32[]{:S(2)}, u32[]{:S(2)}) collective-permute-start(f32[8,128]{1,0:T(8,128)S(1)} %energy.1), channel_id=1, source_target_pairs={{0,2},{1,3},{2,0},{3,1},{4,6},{5,7},{6,4},{7,5},{8,10},{9,11},{10,... | collective-permute-start | bytes 12296 | tf_op jit(solution)/shard_map/ppermute | solution.py:409
  25.4 3.6 %collective-permute-start.3 = (f32[8,128]{1,0:T(8,128)S(1)}, f32[8,128]{1,0:T(8,128)S(1)}, u32[]{:S(2)}, u32[]{:S(2)}) collective-permute-start(f32[8,128]{1,0:T(8,128)S(1)} %energy.1), channel_id=1, source_target_pairs={{0,3},{1,0},{2,1},{3,2},{4,7},{5,4},{6,5},{7,6},{8,11},{9,8},{10,9... | collective-permute-start | bytes 12296 | tf_op jit(solution)/shard_map/ppermute | solution.py:409
  29.0 1.2 %copy-start.1 = (s32[1,32]{1,0:T(1,128)S(1)}, s32[1,32]{1,0:T(1,128)}, u32[]{:S(2)}) copy-start(s32[1,32]{1,0:T(1,128)} %slots_ref.3) | copy-start | bytes 388
  29.1 1.2 %collective-permute-start.4 = (f32[8,128]{1,0:T(8,128)S(1)}, f32[8,128]{1,0:T(8,128)S(1)}, u32[]{:S(2)}, u32[]{:S(2)}) collective-permute-start(f32[8,128]{1,0:T(8,128)S(1)} %add_add_fusion), channel_id=1, source_target_pairs={{0,4},{4,0},{8,12},{12,8},{16,20},{20,16},{24,28},{28,24},{32,36},... | collective-permute-start | bytes 12296 | tf_op jit(solution)/shard_map/ppermute | solution.py:416
  31.8 16.8 %all-to-all-start.1 = ((bf16[16,136,128]{2,1,0:T(8,128)(2,1)}), bf16[16,136,128]{2,1,0:T(8,128)(2,1)}, u32[]{:S(2)}, u32[]{:S(2)}) async-start(bf16[16,136,128]{2,1,0:T(8,128)(2,1)} %shard_map.135), calls=%async_computation.1 | async-start | bytes 1114112 | tf_op jit(solution)/shard_map/all_to_all | solution.py:404
  71.1 1.9 %collective-permute-start.5 = (bf16[16,32,512]{2,1,0:T(8,128)(2,1)S(1)}, bf16[16,32,512]{2,1,0:T(8,128)(2,1)S(1)}, u32[]{:S(2)}, u32[]{:S(2)}) collective-permute-start(bf16[16,32,512]{2,1,0:T(8,128)(2,1)S(1)} %all_to_all.21.own_ref), channel_id=1, source_target_pairs={{0,4},{4,0},{8,12},{12,8},{16,20},{20,16},{24,28},{28,24},{32,36},... | collective-permute-start | bytes 1572872 | tf_op jit(solution)/shard_map/ppermute | solution.py:429
  74.5 19.9 %all-to-all-start.3 = ((bf16[16,32,512]{2,1,0:T(8,128)(2,1)}), bf16[16,32,512]{2,1,0:T(8,128)(2,1)S(1)}, u32[]{:S(2)}, u32[]{:S(2)}) async-start(bf16[16,32,512]{2,1,0:T(8,128)(2,1)} %shard_map.137), calls=%async_computation.3 | async-start | bytes 1048576 | tf_op jit(solution)/shard_map/all_to_all | solution.py:404

commit v3 on v2

--- a/solution.py
+++ b/solution.py
@@ -142,14 +142,12 @@
     stores.wait()
 
 
-def right_kernel(stats_hbm, basis_hbm, out_hbm, stats, basis, y, ah, al, xh, xl, gh, gl, in_sems, out_sems):
-    loads = make_loads(((basis_hbm, basis), (stats_hbm, stats)), in_sems)
+def right_kernel(basis, stats_hbm, out_hbm, stats, y, ah, al, xh, xl, gh, gl, in_sems, out_sems):
+    loads = make_loads(((stats_hbm, stats),), in_sems)
     stores = Stores(out_sems)
-    for load in loads:
-        load.start()
+    loads[0].start()
+    store_split(basis[...].T, xh, xl)
     loads[0].wait()
-    store_split(basis[...].T, xh, xl)
-    loads[1].wait()
     store_split(stats[...], ah, al)
     first_iterate(y, ah, al, xh, xl)
     for _ in range(NS_ITERS - 1):
@@ -194,13 +192,13 @@
     stores.wait()
 
 
-def window_call(kernel, operands, outs, scratch, passes, limit):
+def window_call(kernel, operands, outs, scratch, passes, limit, ready=0):
     hbm = pl.BlockSpec(memory_space=pltpu.HBM)
     n = outs[0].shape[0]
     return pl.pallas_call(
         kernel,
         out_shape=outs,
-        in_specs=[hbm] * len(operands),
+        in_specs=[pl.BlockSpec(memory_space=pltpu.VMEM)] * ready + [hbm] * (len(operands) - ready),
         out_specs=[hbm] * len(outs),
         scratch_shapes=scratch + [pltpu.SemaphoreType.DMA((8,)), pltpu.SemaphoreType.DMA((12,))],
         compiler_params=pltpu.CompilerParams(vmem_limit_bytes=limit),
@@ -218,9 +216,9 @@
 
 def right_call(stats, basis):
     n = stats.shape[0]
-    scratch = [pltpu.VMEM((n, n), F32)] * 3 + [pltpu.VMEM((n, n), BF16)] * 6
+    scratch = [pltpu.VMEM((n, n), F32)] * 2 + [pltpu.VMEM((n, n), BF16)] * 6
     outs = (jax.ShapeDtypeStruct((n, n), F32),)
-    return window_call(right_kernel, (stats, basis), outs, scratch, 21, 65_600_000)[0]
+    return window_call(right_kernel, (basis, stats), outs, scratch, 21, 55_000_000, ready=1)[0]
 
 
 def late_call(half, got, factor, moment, left, right):

time: 96.8 us -> 96.5 us (level)
  transfers between devices with their start and end apart: 8 -> 8, of which waited for: 5 -> 5; matrix products, arithmetic and copies ran while one was open for 0% -> 0% of each run, Pallas kernels for 27% -> 26%
where the time goes in v3:
time: 96.5 us; the launch traced here: 94.8 us
  Pallas kernels  35.5 us (37%)
  blocking collectives  34 us (35%)
  starting transfers between devices  14.6 us (15%)
  waiting for transfers between devices  9.19 us (10%)
    all_to_all x2, blocking collectives, exchange(): return lax.all_to_all(pieces, 'shard', 0, 0, axis_index_groups=same_core)  34 us
    pallas_call x3, Pallas kernels, window_call(): pl.pallas_call(kernel, out_shape=outs, in_specs=[pl.BlockSpec(memory_spac...  24.7 us
    all_to_all x2, starting transfers between devices, exchange(): return lax.all_to_all(pieces, 'shard', 0, 0, axis_index_groups=same_core)  7.99 us
    pallas_call x1, Pallas kernels, step_call(): pl.pallas_call(functools.partial(step_kernel, entries), out_shape=(jax.Sh...  7.31 us
    ppermute x3, starting transfers between devices, shards(): lax.ppermute(energy, 'tensor', [(i, (i + s) % tensor_count) for i in rang...  6.58 us
    all_to_all x2, waiting for transfers between devices, exchange(): return lax.all_to_all(pieces, 'shard', 0, 0, axis_index_groups=same_core)  3.52 us
    pallas_call x2, Pallas kernels, pick_call(): pl.pallas_call(kernel, out_shape=jax.ShapeDtypeStruct(shape, BF16), in_sp...  3.06 us
    ppermute x3, waiting for transfers between devices, shards(): lax.ppermute(energy, 'tensor', [(i, (i + s) % tensor_count) for i in rang...  2.6 us
  transfers between devices with their start and end apart: 8, of which 5 were waited for; matrix products, arithmetic and copies ran while one was open for 0% of the time, Pallas kernels for 26%

profile of v3, /device:TPU:0, one launch (start us, length us, event | category | flops | bytes accessed | tf_op | source)
XLA Modules:
  0.0 94.8 jit_solution(3257664027886870037)
XLA Ops:
  0.6 0.0 copy-start
  0.6 18.8 %all_to_all.20.own_ref = bf16[16,32,512]{2,1,0:T(8,128)(2,1)S(1)} all-to-all(bf16[16,32,512]{2,1,0:T(8,128)(2,1)} %bitcast.14), channel_id=1, replica_groups={{0,8,16,24,32,40,48,56,64,72,80,88,96,104,112,120},{4,12,20,28,36,44,52..., dimensions={0} | all-to-all | bytes 1048576 | tf_op jit(solution)/shard_map/all_to_all | solution.py:402
  19.5 0.0 collective-permute-start
  19.5 0.0 copy-done
  19.5 0.4 energy.1
  19.9 2.0 %collective-permute-start.1 = (f32[8,128]{1,0:T(8,128)S(1)}, f32[8,128]{1,0:T(8,128)S(1)}, u32[]{:S(2)}, u32[]{:S(2)}) collective-permute-start(f32[8,128]{1,0:T(8,128)S(1)} %energy.1), channel_id=1, source_target_pairs={{0,1},{1,2},{2,3},{3,0},{4,5},{5,6},{6,7},{7,4},{8,9},{9,10},{10,1... | collective-permute-start | bytes 12296 | tf_op jit(solution)/shard_map/ppermute | solution.py:407
  21.9 3.6 %collective-permute-start.2 = (f32[8,128]{1,0:T(8,128)S(1)}, f32[8,128]{1,0:T(8,128)S(1)}, u32[]{:S(2)}, u32[]{:S(2)}) collective-permute-start(f32[8,128]{1,0:T(8,128)S(1)} %energy.1), channel_id=1, source_target_pairs={{0,2},{1,3},{2,0},{3,1},{4,6},{5,7},{6,4},{7,5},{8,10},{9,11},{10,... | collective-permute-start | bytes 12296 | tf_op jit(solution)/shard_map/ppermute | solution.py:407
  25.4 1.0 %collective-permute-start.3 = (f32[8,128]{1,0:T(8,128)S(1)}, f32[8,128]{1,0:T(8,128)S(1)}, u32[]{:S(2)}, u32[]{:S(2)}) collective-permute-start(f32[8,128]{1,0:T(8,128)S(1)} %energy.1), channel_id=1, source_target_pairs={{0,3},{1,0},{2,1},{3,2},{4,7},{5,4},{6,5},{7,6},{8,11},{9,8},{10,9... | collective-permute-start | bytes 12296 | tf_op jit(solution)/shard_map/ppermute | solution.py:407
  26.4 0.0 collective-permute-done.1
  26.4 0.6 collective-permute-done.2
  27.1 2.0 %collective-permute-done.3 = f32[8,128]{1,0:T(8,128)S(1)} collective-permute-done((f32[8,128]{1,0:T(8,128)S(1)}, f32[8,128]{1,0:T(8,128)S(1)}, u32[]{:S(2)}, u32[]{:S(2)}) %collective-permute-start.3) | collective-permute-done | bytes 4128 | tf_op jit(solution)/shard_map/ppermute | solution.py:407
  29.0 0.0 copy-start.1
  29.1 0.0 collective-permute-start.4
  29.1 1.2 %collective-permute-done.4 = f32[8,128]{1,0:T(8,128)S(1)} collective-permute-done((f32[8,128]{1,0:T(8,128)S(1)}, f32[8,128]{1,0:T(8,128)S(1)}, u32[]{:S(2)}, u32[]{:S(2)}) %collective-permute-start.4) | collective-permute-done | bytes 4128 | tf_op jit(solution)/shard_map/ppermute | solution.py:414
  30.2 0.0 collective-permute-done.other_ref
  30.2 0.0 copy-done.1
  30.2 1.6 %shard_map.135 = bf16[16,136,128]{2,1,0:T(8,128)(2,1)} custom-call(s32[1,32]{1,0:T(1,128)S(1)} %copy-done.1, bf16[16,32,512]{2,1,0:T(8,128)(2,1)S(1)} %all_to_all.20.own_ref, bf16[16,32,512]{2,1,0:T(8,128)(2,1)S(1)} %collective-permute-done.other_ref, f32[8,128]{1,0:T(8,128)S(1)} %add.15.energy_ref), custom_call_target="tpu_custom_call" | custom-call | bytes 2097152 | tf_op jit(solution)/shard_map/pallas_call | solution.py:376
  31.8 4.2 %all-to-all-start.1 = ((bf16[16,136,128]{2,1,0:T(8,128)(2,1)}), bf16[16,136,128]{2,1,0:T(8,128)(2,1)}, u32[]{:S(2)}, u32[]{:S(2)}) async-start(bf16[16,136,128]{2,1,0:T(8,128)(2,1)} %shard_map.135), calls=%async_computation.1 | async-start | bytes 1114112 | tf_op jit(solution)/shard_map/all_to_all | solution.py:402
  36.1 9.0 %shard_map.136 = (f32[512,512]{1,0:T(8,128)}, f32[512,512]{1,0:T(8,128)}, bf16[512,512]{1,0:T(8,128)(2,1)}, bf16[512,512]{1,0:T(8,128)(2,1)}, bf16[512,512]{1,0:...) custom-call(f32[512,512]{1,0:T(8,128)} %bitcast.18, ...), custom_call_target="tpu_custom_call" | custom-call | flops 4831838208 | bytes 8388608 | tf_op jit(solution)/shard_map/pallas_call | solution.py:198
  45.1 3.5 %all-to-all-done.1.got_hbm = bf16[16,136,128]{2,1,0:T(8,128)(2,1)} async-done(((bf16[16,136,128]{2,1,0:T(8,128)(2,1)}), bf16[16,136,128]{2,1,0:T(8,128)(2,1)}, u32[]{:S(2)}, u32[]{:S(2)}) %all-to-all-start.1) | async-done | bytes 557088 | tf_op jit(solution)/shard_map/all_to_all | solution.py:402
  48.6 7.3 %step.1 = (bf16[16,32,512]{2,1,0:T(8,128)(2,1)}, f32[512,512]{1,0:T(8,128)}, f32[8,128]{1,0:T(8,128)}) custom-call(bf16[16,136,128]{2,1,0:T(8,128)(2,1)} %all-to-all-done.1.got_hbm, bf16[512,512]{1,0:T(8,128)(2,1)} %get-tuple-element.22.lth_hbm, bf16[512,512]{1,0:T(8,128)(2,1)} %get-tuple-element.23.ltl_hbm, bf16[512,512]{1,0:T(8,128)(2,1)} %get-tuple-element.24.rh_hbm, ...), custom_call_target="tpu_custom_call" | custom-call | flops 2952790016 | bytes 7340032 | tf_op jit(solution)/shard_map/step/pallas_call | solution.py:311
  55.9 15.2 %all_to_all.21.own_ref = bf16[16,32,512]{2,1,0:T(8,128)(2,1)S(1)} all-to-all(bf16[16,32,512]{2,1,0:T(8,128)(2,1)} %get-tuple-element.29), channel_id=1, replica_groups={{0,8,16,24,32,40,48,56,64,72,80,88,96,104,112,120},{4,12,20,28,36,44,52..., dimensions={0} | all-to-all | bytes 1048576 | tf_op jit(solution)/shard_map/all_to_all | solution.py:402
  71.1 0.0 copy-start.2
  71.1 0.0 collective-permute-start.5
  71.1 1.9 %collective-permute-done.5.other_ref = bf16[16,32,512]{2,1,0:T(8,128)(2,1)S(1)} collective-permute-done((bf16[16,32,512]{2,1,0:T(8,128)(2,1)S(1)}, bf16[16,32,512]{2,1,0:T(8,128)(2,1)S(1)}, u32[]{:S(2)}, u32[]{:S(2)}) %collective-permute-start.5) | collective-permute-done | bytes 524320 | tf_op jit(solution)/shard_map/ppermute | solution.py:427
  73.0 1.5 %shard_map.137 = bf16[16,32,512]{2,1,0:T(8,128)(2,1)} custom-call(s32[1,32]{1,0:T(1,128)S(1)} %copy-done.1, bf16[16,32,512]{2,1,0:T(8,128)(2,1)S(1)} %all_to_all.21.own_ref, bf16[16,32,512]{2,1,0:T(8,128)(2,1)S(1)} %collective-permute-done.5.other_ref), custom_call_target="tpu_custom_call" | custom-call | bytes 2097152 | tf_op jit(solution)/shard_map/pallas_call | solution.py:376
  74.5 3.8 %all-to-all-start.3 = ((bf16[16,32,512]{2,1,0:T(8,128)(2,1)}), bf16[16,32,512]{2,1,0:T(8,128)(2,1)S(1)}, u32[]{:S(2)}, u32[]{:S(2)}) async-start(bf16[16,32,512]{2,1,0:T(8,128)(2,1)} %shard_map.137), calls=%async_computation.3 | async-start | bytes 1048576 | tf_op jit(solution)/shard_map/all_to_all | solution.py:402
  78.2 0.0 copy-done.2
  78.2 9.1 %shard_map.139 = f32[512,512]{1,0:T(8,128)} custom-call(f32[512,512]{1,0:T(8,128)S(1)} %bitcast.16, f32[512,512]{1,0:T(8,128)} %bitcast.24), custom_call_target="tpu_custom_call" | custom-call | flops 5637144576 | bytes 8388608 | tf_op jit(solution)/shard_map/pallas_call | solution.py:198
  87.4 6.6 %shard_map.138 = (f32[512,512]{1,0:T(8,128)}, f32[512,512]{1,0:T(8,128)}, f32[512,512]{1,0:T(8,128)}, f32[512,512]{1,0:T(8,128)}) custom-call(f32[512,512]{1,0:T(8,128)} %get-tuple-element.30.y_hbm, bf16[16,136,128]{2,1,0:T(8,128)(2,1)} %all-to-all-done.1.got_hbm, f32[8,128]{1,0:T(8,128)} %get-tuple-element.31.factor_hbm, f32[512,512]{1,0:T(8,128)} %bitcast.23, ...), custom_call_target="tpu_custom_call" | custom-call | flops 2952790016 | bytes 8388608 | tf_op jit(solution)/shard_map/pallas_call | solution.py:198
  94.0 0.0 all-to-all-done.3
  94.0 0.8 copy.16
  (2 shorter events, 0.0 us)
Async XLA Ops:
  0.6 18.8 %copy-start = (bf16[512,512]{1,0:T(8,128)(2,1)S(1)}, bf16[512,512]{1,0:T(8,128)(2,1)}, u32[]{:S(2)}) copy-start(bf16[512,512]{1,0:T(8,128)(2,1)} %grads_ref.1) | copy-start | bytes 1572868
  19.5 10.8 %collective-permute-start = (bf16[16,32,512]{2,1,0:T(8,128)(2,1)S(1)}, bf16[16,32,512]{2,1,0:T(8,128)(2,1)S(1)}, u32[]{:S(2)}, u32[]{:S(2)}) collective-permute-start(bf16[16,32,512]{2,1,0:T(8,128)(2,1)S(1)} %all_to_all.20.own_ref), channel_id=1, source_target_pairs={{0,4},{4,0},{8,12},{12,8},{16,20},{20,16},{24,28},{28,24},{32,36},... | collective-permute-start | bytes 1572872 | tf_op jit(solution)/shard_map/ppermute | solution.py:415
  19.9 6.6 %collective-permute-start.1 = (f32[8,128]{1,0:T(8,128)S(1)}, f32[8,128]{1,0:T(8,128)S(1)}, u32[]{:S(2)}, u32[]{:S(2)}) collective-permute-start(f32[8,128]{1,0:T(8,128)S(1)} %energy.1), channel_id=1, source_target_pairs={{0,1},{1,2},{2,3},{3,0},{4,5},{5,6},{6,7},{7,4},{8,9},{9,10},{10,1... | collective-permute-start | bytes 12296 | tf_op jit(solution)/shard_map/ppermute | solution.py:407
  21.9 5.2 %collective-permute-start.2 = (f32[8,128]{1,0:T(8,128)S(1)}, f32[8,128]{1,0:T(8,128)S(1)}, u32[]{:S(2)}, u32[]{:S(2)}) collective-permute-start(f32[8,128]{1,0:T(8,128)S(1)} %energy.1), channel_id=1, source_target_pairs={{0,2},{1,3},{2,0},{3,1},{4,6},{5,7},{6,4},{7,5},{8,10},{9,11},{10,... | collective-permute-start | bytes 12296 | tf_op jit(solution)/shard_map/ppermute | solution.py:407
  25.4 3.6 %collective-permute-start.3 = (f32[8,128]{1,0:T(8,128)S(1)}, f32[8,128]{1,0:T(8,128)S(1)}, u32[]{:S(2)}, u32[]{:S(2)}) collective-permute-start(f32[8,128]{1,0:T(8,128)S(1)} %energy.1), channel_id=1, source_target_pairs={{0,3},{1,0},{2,1},{3,2},{4,7},{5,4},{6,5},{7,6},{8,11},{9,8},{10,9... | collective-permute-start | bytes 12296 | tf_op jit(solution)/shard_map/ppermute | solution.py:407
  29.0 1.2 %copy-start.1 = (s32[1,32]{1,0:T(1,128)S(1)}, s32[1,32]{1,0:T(1,128)}, u32[]{:S(2)}) copy-start(s32[1,32]{1,0:T(1,128)} %slots_ref.3) | copy-start | bytes 388
  29.1 1.2 %collective-permute-start.4 = (f32[8,128]{1,0:T(8,128)S(1)}, f32[8,128]{1,0:T(8,128)S(1)}, u32[]{:S(2)}, u32[]{:S(2)}) collective-permute-start(f32[8,128]{1,0:T(8,128)S(1)} %add_add_fusion), channel_id=1, source_target_pairs={{0,4},{4,0},{8,12},{12,8},{16,20},{20,16},{24,28},{28,24},{32,36},... | collective-permute-start | bytes 12296 | tf_op jit(solution)/shard_map/ppermute | solution.py:414
  31.8 16.8 %all-to-all-start.1 = ((bf16[16,136,128]{2,1,0:T(8,128)(2,1)}), bf16[16,136,128]{2,1,0:T(8,128)(2,1)}, u32[]{:S(2)}, u32[]{:S(2)}) async-start(bf16[16,136,128]{2,1,0:T(8,128)(2,1)} %shard_map.135), calls=%async_computation.1 | async-start | bytes 1114112 | tf_op jit(solution)/shard_map/all_to_all | solution.py:402
  71.1 7.1 %copy-start.2 = (f32[1,512,512]{2,1,0:T(8,128)S(1)}, f32[1,512,512]{2,1,0:T(8,128)}, u32[]{:S(2)}) copy-start(f32[1,512,512]{2,1,0:T(8,128)} %param.15) | copy-start | bytes 3145732
  71.1 1.9 %collective-permute-start.5 = (bf16[16,32,512]{2,1,0:T(8,128)(2,1)S(1)}, bf16[16,32,512]{2,1,0:T(8,128)(2,1)S(1)}, u32[]{:S(2)}, u32[]{:S(2)}) collective-permute-start(bf16[16,32,512]{2,1,0:T(8,128)(2,1)S(1)} %all_to_all.21.own_ref), channel_id=1, source_target_pairs={{0,4},{4,0},{8,12},{12,8},{16,20},{20,16},{24,28},{28,24},{32,36},... | collective-permute-start | bytes 1572872 | tf_op jit(solution)/shard_map/ppermute | solution.py:427
  74.5 19.5 %all-to-all-start.3 = ((bf16[16,32,512]{2,1,0:T(8,128)(2,1)}), bf16[16,32,512]{2,1,0:T(8,128)(2,1)S(1)}, u32[]{:S(2)}, u32[]{:S(2)}) async-start(bf16[16,32,512]{2,1,0:T(8,128)(2,1)} %shard_map.137), calls=%async_computation.3 | async-start | bytes 1048576 | tf_op jit(solution)/shard_map/all_to_all | solution.py:402

commit v4 on v3

--- a/solution.py
+++ b/solution.py
@@ -364,21 +364,31 @@
         out_ref[chip, out_ref.shape[1] - 8 :, :] = packed
 
 
-def return_kernel(slots_ref, own_ref, other_ref, out_ref):
+def return_kernel(slots_ref, own_ref, other_ref, out_ref, sems):
     core = lax.rem(lax.axis_index("shard"), 2)
     for i in range(own_ref.shape[0]):
         slot = slots_ref[0, 2 * i + core]
         mine = lax.rem(slot, 2) == core
-        out_ref[i] = jnp.where(mine, own_ref[slot // 2], other_ref[slot // 2])
-
-
-def pick_call(kernel, shape, scratch, operands):
+
+        @pl.when(mine)
+        def _():
+            pltpu.make_async_copy(own_ref.at[slot // 2], out_ref.at[i], sems.at[i]).start()
+
+        @pl.when(jnp.logical_not(mine))
+        def _():
+            pltpu.make_async_copy(other_ref.at[slot // 2], out_ref.at[i], sems.at[i]).start()
+
+    for i in range(own_ref.shape[0]):
+        pltpu.make_async_copy(own_ref.at[i], out_ref.at[i], sems.at[i]).wait()
+
+
+def pick_call(kernel, shape, scratch, operands, space=pltpu.VMEM):
     return pl.pallas_call(
         kernel,
         out_shape=jax.ShapeDtypeStruct(shape, BF16),
         in_specs=[pl.BlockSpec(memory_space=pltpu.SMEM)]
         + [pl.BlockSpec(memory_space=pltpu.VMEM)] * (len(operands) - 1),
-        out_specs=pl.BlockSpec(memory_space=pltpu.VMEM),
+        out_specs=pl.BlockSpec(memory_space=space),
         scratch_shapes=scratch,
         compiler_params=pltpu.CompilerParams(vmem_limit_bytes=8 << 20),
         cost_estimate=pl.CostEstimate(flops=0, bytes_accessed=1 << 21, transcendentals=0),
@@ -425,7 +435,13 @@
     returned = exchange(update)
     right_basis_new = right_call(right_stats, right_basis)
     other = lax.ppermute(returned, "shard", swap)
-    picked = pick_call(return_kernel, (chips, rows, size), [], (assignment, returned, other))
+    picked = pick_call(
+        return_kernel,
+        (chips, rows, size),
+        [pltpu.SemaphoreType.DMA((chips,))],
+        (assignment, returned, other),
+        pltpu.HBM,
+    )
     update_out = exchange(picked).reshape(size, size)
     left_basis_new, moment_new, left_new, right_new = late_call(left_half, got, factor, moment, left_stats, right_stats)
 

time: 96.5 us -> 96.5 us (level)
  no operation moved by 1% of the time
where the time goes in v4:
time: 96.5 us; the launch traced here: 94.9 us
  Pallas kernels  35.5 us (37%)
  blocking collectives  34 us (35%)
  starting transfers between devices  14.6 us (15%)
  waiting for transfers between devices  9.19 us (10%)
    all_to_all x2, blocking collectives, exchange(): return lax.all_to_all(pieces, 'shard', 0, 0, axis_index_groups=same_core)  34 us
    pallas_call x3, Pallas kernels, window_call(): pl.pallas_call(kernel, out_shape=outs, in_specs=[pl.BlockSpec(memory_spac...  24.7 us
    all_to_all x2, starting transfers between devices, exchange(): return lax.all_to_all(pieces, 'shard', 0, 0, axis_index_groups=same_core)  8 us
    pallas_call x1, Pallas kernels, step_call(): pl.pallas_call(functools.partial(step_kernel, entries), out_shape=(jax.Sh...  7.31 us
    ppermute x3, starting transfers between devices, shards(): lax.ppermute(energy, 'tensor', [(i, (i + s) % tensor_count) for i in rang...  6.58 us
    all_to_all x2, waiting for transfers between devices, exchange(): return lax.all_to_all(pieces, 'shard', 0, 0, axis_index_groups=same_core)  3.52 us
    pallas_call x2, Pallas kernels, pick_call(): pl.pallas_call(kernel, out_shape=jax.ShapeDtypeStruct(shape, BF16), in_sp...  3.09 us
    ppermute x3, waiting for transfers between devices, shards(): lax.ppermute(energy, 'tensor', [(i, (i + s) % tensor_count) for i in rang...  2.6 us
  transfers between devices with their start and end apart: 8, of which 5 were waited for; matrix products, arithmetic and copies ran while one was open for 0% of the time, Pallas kernels for 26%

profile of v4, /device:TPU:0, one launch (start us, length us, event | category | flops | bytes accessed | tf_op | source)
XLA Modules:
  0.0 94.9 jit_solution(9485960051158490486)
XLA Ops:
  0.6 0.0 copy-start
  0.6 18.8 %all_to_all.20.own_ref = bf16[16,32,512]{2,1,0:T(8,128)(2,1)S(1)} all-to-all(bf16[16,32,512]{2,1,0:T(8,128)(2,1)} %bitcast.14), channel_id=1, replica_groups={{0,8,16,24,32,40,48,56,64,72,80,88,96,104,112,120},{4,12,20,28,36,44,52..., dimensions={0} | all-to-all | bytes 1048576 | tf_op jit(solution)/shard_map/all_to_all | solution.py:412
  19.5 0.0 collective-permute-start
  19.5 0.0 copy-done
  19.5 0.4 energy.1
  19.9 2.0 %collective-permute-start.1 = (f32[8,128]{1,0:T(8,128)S(1)}, f32[8,128]{1,0:T(8,128)S(1)}, u32[]{:S(2)}, u32[]{:S(2)}) collective-permute-start(f32[8,128]{1,0:T(8,128)S(1)} %energy.1), channel_id=1, source_target_pairs={{0,1},{1,2},{2,3},{3,0},{4,5},{5,6},{6,7},{7,4},{8,9},{9,10},{10,1... | collective-permute-start | bytes 12296 | tf_op jit(solution)/shard_map/ppermute | solution.py:417
  21.9 3.6 %collective-permute-start.2 = (f32[8,128]{1,0:T(8,128)S(1)}, f32[8,128]{1,0:T(8,128)S(1)}, u32[]{:S(2)}, u32[]{:S(2)}) collective-permute-start(f32[8,128]{1,0:T(8,128)S(1)} %energy.1), channel_id=1, source_target_pairs={{0,2},{1,3},{2,0},{3,1},{4,6},{5,7},{6,4},{7,5},{8,10},{9,11},{10,... | collective-permute-start | bytes 12296 | tf_op jit(solution)/shard_map/ppermute | solution.py:417
  25.4 1.0 %collective-permute-start.3 = (f32[8,128]{1,0:T(8,128)S(1)}, f32[8,128]{1,0:T(8,128)S(1)}, u32[]{:S(2)}, u32[]{:S(2)}) collective-permute-start(f32[8,128]{1,0:T(8,128)S(1)} %energy.1), channel_id=1, source_target_pairs={{0,3},{1,0},{2,1},{3,2},{4,7},{5,4},{6,5},{7,6},{8,11},{9,8},{10,9... | collective-permute-start | bytes 12296 | tf_op jit(solution)/shard_map/ppermute | solution.py:417
  26.4 0.0 collective-permute-done.1
  26.4 0.6 collective-permute-done.2
  27.1 2.0 %collective-permute-done.3 = f32[8,128]{1,0:T(8,128)S(1)} collective-permute-done((f32[8,128]{1,0:T(8,128)S(1)}, f32[8,128]{1,0:T(8,128)S(1)}, u32[]{:S(2)}, u32[]{:S(2)}) %collective-permute-start.3) | collective-permute-done | bytes 4128 | tf_op jit(solution)/shard_map/ppermute | solution.py:417
  29.0 0.0 copy-start.1
  29.1 0.0 collective-permute-start.4
  29.1 1.2 %collective-permute-done.4 = f32[8,128]{1,0:T(8,128)S(1)} collective-permute-done((f32[8,128]{1,0:T(8,128)S(1)}, f32[8,128]{1,0:T(8,128)S(1)}, u32[]{:S(2)}, u32[]{:S(2)}) %collective-permute-start.4) | collective-permute-done | bytes 4128 | tf_op jit(solution)/shard_map/ppermute | solution.py:424
  30.2 0.0 collective-permute-done.other_ref
  30.2 0.0 copy-done.1
  30.2 1.6 %shard_map.135 = bf16[16,136,128]{2,1,0:T(8,128)(2,1)} custom-call(s32[1,32]{1,0:T(1,128)S(1)} %copy-done.1, bf16[16,32,512]{2,1,0:T(8,128)(2,1)S(1)} %all_to_all.20.own_ref, bf16[16,32,512]{2,1,0:T(8,128)(2,1)S(1)} %collective-permute-done.other_ref, f32[8,128]{1,0:T(8,128)S(1)} %add.15.energy_ref), custom_call_target="tpu_custom_call" | custom-call | bytes 2097152 | tf_op jit(solution)/shard_map/pallas_call | solution.py:386
  31.8 4.2 %all-to-all-start.1 = ((bf16[16,136,128]{2,1,0:T(8,128)(2,1)}), bf16[16,136,128]{2,1,0:T(8,128)(2,1)}, u32[]{:S(2)}, u32[]{:S(2)}) async-start(bf16[16,136,128]{2,1,0:T(8,128)(2,1)} %shard_map.135), calls=%async_computation.1 | async-start | bytes 1114112 | tf_op jit(solution)/shard_map/all_to_all | solution.py:412
  36.1 9.0 %shard_map.136 = (f32[512,512]{1,0:T(8,128)}, f32[512,512]{1,0:T(8,128)}, bf16[512,512]{1,0:T(8,128)(2,1)}, bf16[512,512]{1,0:T(8,128)(2,1)}, bf16[512,512]{1,0:...) custom-call(f32[512,512]{1,0:T(8,128)} %bitcast.18, ...), custom_call_target="tpu_custom_call" | custom-call | flops 4831838208 | bytes 8388608 | tf_op jit(solution)/shard_map/pallas_call | solution.py:198
  45.1 3.5 %all-to-all-done.1.got_hbm = bf16[16,136,128]{2,1,0:T(8,128)(2,1)} async-done(((bf16[16,136,128]{2,1,0:T(8,128)(2,1)}), bf16[16,136,128]{2,1,0:T(8,128)(2,1)}, u32[]{:S(2)}, u32[]{:S(2)}) %all-to-all-start.1) | async-done | bytes 557088 | tf_op jit(solution)/shard_map/all_to_all | solution.py:412
  48.6 7.3 %step.1 = (bf16[16,32,512]{2,1,0:T(8,128)(2,1)}, f32[512,512]{1,0:T(8,128)}, f32[8,128]{1,0:T(8,128)}) custom-call(bf16[16,136,128]{2,1,0:T(8,128)(2,1)} %all-to-all-done.1.got_hbm, bf16[512,512]{1,0:T(8,128)(2,1)} %get-tuple-element.22.lth_hbm, bf16[512,512]{1,0:T(8,128)(2,1)} %get-tuple-element.23.ltl_hbm, bf16[512,512]{1,0:T(8,128)(2,1)} %get-tuple-element.24.rh_hbm, ...), custom_call_target="tpu_custom_call" | custom-call | flops 2952790016 | bytes 7340032 | tf_op jit(solution)/shard_map/step/pallas_call | solution.py:311
  55.9 15.2 %all_to_all.21.own_ref = bf16[16,32,512]{2,1,0:T(8,128)(2,1)S(1)} all-to-all(bf16[16,32,512]{2,1,0:T(8,128)(2,1)} %get-tuple-element.29), channel_id=1, replica_groups={{0,8,16,24,32,40,48,56,64,72,80,88,96,104,112,120},{4,12,20,28,36,44,52..., dimensions={0} | all-to-all | bytes 1048576 | tf_op jit(solution)/shard_map/all_to_all | solution.py:412
  71.1 0.0 copy-start.2
  71.1 0.0 collective-permute-start.5
  71.1 1.9 %collective-permute-done.5.other_ref = bf16[16,32,512]{2,1,0:T(8,128)(2,1)S(1)} collective-permute-done((bf16[16,32,512]{2,1,0:T(8,128)(2,1)S(1)}, bf16[16,32,512]{2,1,0:T(8,128)(2,1)S(1)}, u32[]{:S(2)}, u32[]{:S(2)}) %collective-permute-start.5) | collective-permute-done | bytes 524320 | tf_op jit(solution)/shard_map/ppermute | solution.py:437
  73.0 1.5 %shard_map.137 = bf16[16,32,512]{2,1,0:T(8,128)(2,1)} custom-call(s32[1,32]{1,0:T(1,128)S(1)} %copy-done.1, bf16[16,32,512]{2,1,0:T(8,128)(2,1)S(1)} %all_to_all.21.own_ref, bf16[16,32,512]{2,1,0:T(8,128)(2,1)S(1)} %collective-permute-done.5.other_ref), custom_call_target="tpu_custom_call" | custom-call | bytes 2097152 | tf_op jit(solution)/shard_map/pallas_call | solution.py:386
  74.5 3.8 %all-to-all-start.3 = ((bf16[16,32,512]{2,1,0:T(8,128)(2,1)}), bf16[16,32,512]{2,1,0:T(8,128)(2,1)S(1)}, u32[]{:S(2)}, u32[]{:S(2)}) async-start(bf16[16,32,512]{2,1,0:T(8,128)(2,1)} %shard_map.137), calls=%async_computation.3 | async-start | bytes 1048576 | tf_op jit(solution)/shard_map/all_to_all | solution.py:412
  78.3 0.0 copy-done.2
  78.3 9.1 %shard_map.139 = f32[512,512]{1,0:T(8,128)} custom-call(f32[512,512]{1,0:T(8,128)S(1)} %bitcast.16, f32[512,512]{1,0:T(8,128)} %bitcast.24), custom_call_target="tpu_custom_call" | custom-call | flops 5637144576 | bytes 8388608 | tf_op jit(solution)/shard_map/pallas_call | solution.py:198
  87.4 6.6 %shard_map.138 = (f32[512,512]{1,0:T(8,128)}, f32[512,512]{1,0:T(8,128)}, f32[512,512]{1,0:T(8,128)}, f32[512,512]{1,0:T(8,128)}) custom-call(f32[512,512]{1,0:T(8,128)} %get-tuple-element.30.y_hbm, bf16[16,136,128]{2,1,0:T(8,128)(2,1)} %all-to-all-done.1.got_hbm, f32[8,128]{1,0:T(8,128)} %get-tuple-element.31.factor_hbm, f32[512,512]{1,0:T(8,128)} %bitcast.23, ...), custom_call_target="tpu_custom_call" | custom-call | flops 2952790016 | bytes 8388608 | tf_op jit(solution)/shard_map/pallas_call | solution.py:198
  94.1 0.0 all-to-all-done.3
  94.1 0.8 copy.16
  (2 shorter events, 0.0 us)
Async XLA Ops:
  0.6 18.8 %copy-start = (bf16[512,512]{1,0:T(8,128)(2,1)S(1)}, bf16[512,512]{1,0:T(8,128)(2,1)}, u32[]{:S(2)}) copy-start(bf16[512,512]{1,0:T(8,128)(2,1)} %grads_ref.1) | copy-start | bytes 1572868
  19.5 10.8 %collective-permute-start = (bf16[16,32,512]{2,1,0:T(8,128)(2,1)S(1)}, bf16[16,32,512]{2,1,0:T(8,128)(2,1)S(1)}, u32[]{:S(2)}, u32[]{:S(2)}) collective-permute-start(bf16[16,32,512]{2,1,0:T(8,128)(2,1)S(1)} %all_to_all.20.own_ref), channel_id=1, source_target_pairs={{0,4},{4,0},{8,12},{12,8},{16,20},{20,16},{24,28},{28,24},{32,36},... | collective-permute-start | bytes 1572872 | tf_op jit(solution)/shard_map/ppermute | solution.py:425
  19.9 6.6 %collective-permute-start.1 = (f32[8,128]{1,0:T(8,128)S(1)}, f32[8,128]{1,0:T(8,128)S(1)}, u32[]{:S(2)}, u32[]{:S(2)}) collective-permute-start(f32[8,128]{1,0:T(8,128)S(1)} %energy.1), channel_id=1, source_target_pairs={{0,1},{1,2},{2,3},{3,0},{4,5},{5,6},{6,7},{7,4},{8,9},{9,10},{10,1... | collective-permute-start | bytes 12296 | tf_op jit(solution)/shard_map/ppermute | solution.py:417
  21.9 5.2 %collective-permute-start.2 = (f32[8,128]{1,0:T(8,128)S(1)}, f32[8,128]{1,0:T(8,128)S(1)}, u32[]{:S(2)}, u32[]{:S(2)}) collective-permute-start(f32[8,128]{1,0:T(8,128)S(1)} %energy.1), channel_id=1, source_target_pairs={{0,2},{1,3},{2,0},{3,1},{4,6},{5,7},{6,4},{7,5},{8,10},{9,11},{10,... | collective-permute-start | bytes 12296 | tf_op jit(solution)/shard_map/ppermute | solution.py:417
  25.4 3.6 %collective-permute-start.3 = (f32[8,128]{1,0:T(8,128)S(1)}, f32[8,128]{1,0:T(8,128)S(1)}, u32[]{:S(2)}, u32[]{:S(2)}) collective-permute-start(f32[8,128]{1,0:T(8,128)S(1)} %energy.1), channel_id=1, source_target_pairs={{0,3},{1,0},{2,1},{3,2},{4,7},{5,4},{6,5},{7,6},{8,11},{9,8},{10,9... | collective-permute-start | bytes 12296 | tf_op jit(solution)/shard_map/ppermute | solution.py:417
  29.0 1.2 %copy-start.1 = (s32[1,32]{1,0:T(1,128)S(1)}, s32[1,32]{1,0:T(1,128)}, u32[]{:S(2)}) copy-start(s32[1,32]{1,0:T(1,128)} %slots_ref.3) | copy-start | bytes 388
  29.1 1.2 %collective-permute-start.4 = (f32[8,128]{1,0:T(8,128)S(1)}, f32[8,128]{1,0:T(8,128)S(1)}, u32[]{:S(2)}, u32[]{:S(2)}) collective-permute-start(f32[8,128]{1,0:T(8,128)S(1)} %add_add_fusion), channel_id=1, source_target_pairs={{0,4},{4,0},{8,12},{12,8},{16,20},{20,16},{24,28},{28,24},{32,36},... | collective-permute-start | bytes 12296 | tf_op jit(solution)/shard_map/ppermute | solution.py:424
  31.8 16.8 %all-to-all-start.1 = ((bf16[16,136,128]{2,1,0:T(8,128)(2,1)}), bf16[16,136,128]{2,1,0:T(8,128)(2,1)}, u32[]{:S(2)}, u32[]{:S(2)}) async-start(bf16[16,136,128]{2,1,0:T(8,128)(2,1)} %shard_map.135), calls=%async_computation.1 | async-start | bytes 1114112 | tf_op jit(solution)/shard_map/all_to_all | solution.py:412
  71.1 7.2 %copy-start.2 = (f32[1,512,512]{2,1,0:T(8,128)S(1)}, f32[1,512,512]{2,1,0:T(8,128)}, u32[]{:S(2)}) copy-start(f32[1,512,512]{2,1,0:T(8,128)} %param.15) | copy-start | bytes 3145732
  71.1 1.9 %collective-permute-start.5 = (bf16[16,32,512]{2,1,0:T(8,128)(2,1)S(1)}, bf16[16,32,512]{2,1,0:T(8,128)(2,1)S(1)}, u32[]{:S(2)}, u32[]{:S(2)}) collective-permute-start(bf16[16,32,512]{2,1,0:T(8,128)(2,1)S(1)} %all_to_all.21.own_ref), channel_id=1, source_target_pairs={{0,4},{4,0},{8,12},{12,8},{16,20},{20,16},{24,28},{28,24},{32,36},... | collective-permute-start | bytes 1572872 | tf_op jit(solution)/shard_map/ppermute | solution.py:437
  74.5 19.5 %all-to-all-start.3 = ((bf16[16,32,512]{2,1,0:T(8,128)(2,1)}), bf16[16,32,512]{2,1,0:T(8,128)(2,1)S(1)}, u32[]{:S(2)}, u32[]{:S(2)}) async-start(bf16[16,32,512]{2,1,0:T(8,128)(2,1)} %shard_map.137), calls=%async_computation.3 | async-start | bytes 1048576 | tf_op jit(solution)/shard_map/all_to_all | solution.py:412
